TPU v7x, 32 devices: a whole 2x2x4 slice. The times are simulated.
32 devices in a mesh: row: 4 (over z), col: 8 (over y, x, core).
Axes of the slice: x: 2, y: 2, z: 4, core: 2. Of those that a mesh axis runs over, the one named last changes fastest.
Arguments:
- strain: bfloat16 [256, 33280], P(('row', 'col')), may hold values from -6 to 6
- file_channels: int32 [256], P(('row', 'col')), may hold values from 0 to 127, as said below
- file_counts: int32 [32], P(('row', 'col')), may hold values from 0 to 8, as said below
- window_start: int32 [32], P(('row', 'col')), may hold values from 0 to 512
Outputs:
- correlations: bfloat16 [128, 128, 1024], P('row', 'col')
Inputs may be any that keep to these rules, and one draw needn't show every extreme that they name: `file_channels`: the first file_counts[d] slots of file d are live. The live slots of the 4 files with one col index hold, each exactly once, the channels g whose owner ((g // 4) // 8, (g // 4) % 8) has that col index; dead slots hold arbitrary channel numbers. One file holds at most 2 channels of one owner, and exactly 2 for some file and owner in every group of files with one col index. `file_counts`: in every group of files with one col index some file has all 8 slots live.
All inputs are finite; a program needn't handle non-finite values.
Results may differ from a plain program's by a relative error of at most 0.0076.
Values may be sent and summed in bfloat16 or wider, within the bound.
A program may use at most 128 MiB of HBM per device.

v0:
```python
import functools
import math

import jax
import jax.numpy as jnp
import numpy as np
from jax import lax
from jax.experimental import pallas as pl
from jax.experimental.pallas import tpu as pltpu
from jax.sharding import PartitionSpec as P

NF = 2048
NT = 4096
LAGS = 1024
SEGS = 8
CH_DEV = 4
CAP = 2
SMOOTH = 32
EDGE = 128
N1 = 16
N2 = NT // N1
F2 = NF // N1
HALF = LAGS // 2
PAIR = 2 * F2
STEPS = NF // PAIR
TILE = 256
TILES = 2 * HALF // TILE
GROUP = 2
MESH = pl.DeviceIdType.MESH


def forward_tables():
    n2 = np.arange(N2)
    f1 = np.arange(N1)
    f2 = np.arange(F2)
    angle = 2 * np.pi * (np.outer(f1, n2) % NT) / NT
    twiddle = np.stack([np.cos(angle), -np.sin(angle)]).astype(np.float32)
    angle = 2 * np.pi * (np.outer(n2, f2) % N2) / N2
    c, s = np.cos(angle), np.sin(angle)
    second = np.block([[c, -s], [s, c]]).astype(np.float32)
    high = second.astype(jnp.bfloat16)
    low = (second - high.astype(np.float32)).astype(jnp.bfloat16)
    f = f1[:, None] + N1 * f2[None, :]
    distance = np.minimum(f + 0.5, NF - f - 0.5)
    taper = np.sin(0.5 * np.pi * np.minimum(distance / EDGE, 1.0)) ** 2
    turn = np.pi * f / NT
    shape = np.stack([taper, np.cos(turn), -np.sin(turn)]).astype(np.float32)
    return twiddle, high, low, shape


def lag_tables():
    m2 = 2 * np.arange(HALF) + 1
    f1 = np.arange(N1)
    f2 = N1 * np.arange(F2)
    a = np.pi * (np.outer(f1, m2) % (2 * NT)) / NT
    b = np.pi * (np.outer(f2, m2) % (2 * NT)) / NT
    first = np.stack([np.cos(a), np.sin(a)]).astype(np.float32)
    second = np.stack([np.cos(b), np.sin(b)]).astype(np.float32)
    return first, second


def shifted(value, lanes, amount):
    rolled = pltpu.roll(value, amount % F2, 1)
    source = lanes - amount
    return jnp.where((source >= 0) & (source < F2), rolled, 0.0)


def greet(axes):
    barrier = pltpu.get_barrier_semaphore()
    count = 0
    for axis in axes:
        size, me = lax.axis_size(axis), lax.axis_index(axis)
        for d in range(1, size):
            pl.semaphore_signal(barrier, inc=1, device_id={axis: lax.rem(me + d, size)}, device_id_type=MESH)
            count += 1
    pl.semaphore_wait(barrier, count)


def spectra_kernel(out_ref, *refs):
    sources, rest = refs[:6], refs[6:]
    row_ref, col_ref, w_ref = rest[:3]
    tw_ref, hi_ref, lo_ref, shape_ref, first_ref, second_ref = consts = rest[3:9]
    got, x_ref, z_ref, send_sem, recv_sem, const_sem = rest[9:]
    loads = [pltpu.make_async_copy(f, t, const_sem.at[k]) for k, (f, t) in enumerate(zip(sources, consts))]
    for load in loads[::-1]:
        load.start()
    size, me = lax.axis_size("row"), lax.axis_index("row")
    greet(("row",))

    def copy_of(d):
        peer = lax.rem(me + d, size)
        return pltpu.make_async_remote_copy(
            src_ref=out_ref.at[peer],
            dst_ref=got.at[d],
            send_sem=send_sem.at[d],
            recv_sem=recv_sem.at[d],
            device_id={"row": peer},
            device_id_type=MESH,
        )

    copies = [copy_of(d) for d in range(1, size)]
    for copy in copies:
        copy.start()
    got[0] = out_ref[me]
    for load in loads:
        load.wait()
    for k in range(HALF // TILE):
        lane = slice(k * TILE, (k + 1) * TILE)
        bc, bs = second_ref[0, :, lane], second_ref[1, :, lane]
        for f1 in range(N1):
            ac, as_ = first_ref[0, f1 : f1 + 1, lane], first_ref[1, f1 : f1 + 1, lane]
            t, at = f1 * F2 // PAIR, slice(f1 * F2 % PAIR, f1 * F2 % PAIR + F2)
            w_ref[t, k, at, :] = (ac * bc - as_ * bs).astype(jnp.bfloat16)
            w_ref[t, HALF // TILE + k, at, :] = (-(as_ * bc + ac * bs)).astype(jnp.bfloat16)
    for copy in copies:
        copy.wait()
    rows = x_ref.shape[0]
    slots = [(d, k) for d in range(size) for k in range(CAP)]
    label = [got[d, k, :, NT:].astype(jnp.float32) for d, k in slots]
    for ch in range(rows // SEGS):
        chosen = [v == np.float32(ch) for v in label]
        for h in range(0, NT, 128):
            total = None
            for (d, k), mask in zip(slots, chosen):
                term = jnp.where(mask, got[d, k, :, h : h + 128].astype(jnp.float32), 0.0)
                total = term if total is None else total + term
            x_ref[ch * SEGS : (ch + 1) * SEGS, h : h + 128] = total
    cosines = np.cos(2 * np.pi * np.arange(N1) / N1)
    sines = np.sin(2 * np.pi * np.arange(N1) / N1)

    def combine(values, weights):
        total = None
        for v, w in zip(values, weights):
            if abs(w) < 1e-9:
                continue
            term = v if abs(w - 1) < 1e-9 else (-v if abs(w + 1) < 1e-9 else v * np.float32(w))
            total = term if total is None else total + term
        return total

    for h in range(0, N2, 128):
        xs = [x_ref[:, k * N2 + h : k * N2 + h + 128] for k in range(N1)]
        even = [xs[k] + xs[k + N1 // 2] for k in range(N1 // 2)]
        odd = [xs[k] - xs[k + N1 // 2] for k in range(N1 // 2)]
        for f in range(N1 // 2 + 1):
            src = even if f % 2 == 0 else odd
            re = combine(src, [cosines[f * k % N1] for k in range(N1 // 2)])
            im = combine(src, [-sines[f * k % N1] for k in range(N1 // 2)])
            for f1, sign in {f: 1.0, (N1 - f) % N1: -1.0}.items() if f not in (0, N1 // 2) else ((f, 1.0),):
                tc = tw_ref[0, f1 : f1 + 1, h : h + 128]
                ts = tw_ref[1, f1 : f1 + 1, h : h + 128]
                if im is None:
                    zr, zi = re * tc, re * ts
                else:
                    i = im if sign > 0 else -im
                    zr, zi = re * tc - i * ts, re * ts + i * tc
                z_ref[f1 * rows : (f1 + 1) * rows, h : h + 128] = zr
                z_ref[f1 * rows : (f1 + 1) * rows, N2 + h : N2 + h + 128] = zi
    z = z_ref[...]
    zh = z.astype(jnp.bfloat16)
    zl = (z - zh.astype(jnp.float32)).astype(jnp.bfloat16)
    dot = functools.partial(jnp.dot, preferred_element_type=jnp.float32)
    z_ref[:, : 2 * F2] = dot(zh, hi_ref[...]) + dot(zl, hi_ref[...]) + dot(zh, lo_ref[...])

    lanes = lax.broadcasted_iota(jnp.int32, (rows, F2), 1)
    part = lambda f1, c: z_ref[f1 * rows : (f1 + 1) * rows, c * F2 : (c + 1) * F2]
    power = []
    for f1 in range(N1):
        re, im = part(f1, 0), part(f1, 1)
        power.append(re * re + im * im)
    prefix, suffix = [power[0]], [power[-1]]
    for k in range(1, N1):
        prefix.append(prefix[-1] + power[k])
        suffix.append(suffix[-1] + power[N1 - 1 - k])
    suffix = suffix[::-1]
    total = prefix[-1]
    reach = SMOOTH // N1
    middle = total
    for k in range(1, reach):
        middle = middle + shifted(total, lanes, k) + shifted(total, lanes, -k)
    for f1 in range(N1):
        window = middle + shifted(suffix[f1], lanes, reach) + shifted(prefix[f1], lanes, -reach)
        scale = shape_ref[0, f1 : f1 + 1] * lax.rsqrt(window * (1.0 / (2 * SMOOTH + 1)) + 1e-06)
        re, im = part(f1, 0) * scale, part(f1, 1) * scale
        tc, ts = shape_ref[1, f1 : f1 + 1], shape_ref[2, f1 : f1 + 1]
        tr, ti = re * tc - im * ts, re * ts + im * tc
        for ch in range(rows // SEGS):
            own = slice(ch * SEGS, (ch + 1) * SEGS)
            t, at = f1 * F2 // PAIR, slice(f1 * F2 % PAIR, f1 * F2 % PAIR + F2)
            col_ref[t, ch, :, at] = jnp.concatenate([re[own], im[own]], axis=0).astype(jnp.bfloat16)
            row_ref[t, ch, :, at] = jnp.concatenate([tr[own], ti[own]], axis=0).astype(jnp.bfloat16)


def spectra_of(outgoing):
    size = outgoing.shape[0]
    consts = [jnp.asarray(t) for t in forward_tables() + lag_tables()]
    rows = CH_DEV * SEGS
    shape = jax.ShapeDtypeStruct((STEPS, CH_DEV, 2 * SEGS, PAIR), jnp.bfloat16)
    return pl.pallas_call(
        spectra_kernel,
        out_shape=(shape, shape, jax.ShapeDtypeStruct((STEPS, TILES, PAIR, TILE), jnp.bfloat16)),
        in_specs=[pl.BlockSpec(memory_space=pltpu.VMEM)] + [pl.BlockSpec(memory_space=pl.ANY)] * len(consts),
        out_specs=[pl.BlockSpec(memory_space=pltpu.VMEM)] * 3,
        scratch_shapes=[pltpu.VMEM(t.shape, t.dtype) for t in consts]
        + [
            pltpu.VMEM(outgoing.shape, jnp.bfloat16),
            pltpu.VMEM((rows, NT), jnp.float32),
            pltpu.VMEM((N1 * rows, 2 * N2), jnp.float32),
            pltpu.SemaphoreType.DMA((size,)),
            pltpu.SemaphoreType.DMA((size,)),
            pltpu.SemaphoreType.DMA((len(consts),)),
        ],
        compiler_params=pltpu.CompilerParams(
            vmem_limit_bytes=48 << 20, collective_id=0, has_side_effects=True
        ),
    )(outgoing, *consts)


def tree(terms):
    while len(terms) > 1:
        terms = [terms[k] + terms[k + 1] for k in range(0, len(terms), 2)]
    return terms[0]


def correlate_kernel(
    row_ref, col_ref, w_ref, flip_ref, out_hbm, row_all, col_all, a32, b32, b_ref, cross, acc, out_ref, sems, out_sem
):
    row_total = row_all.shape[1] * CH_DEV
    col_total = col_all.shape[1] * CH_DEV
    share = row_total // TILES
    greet(("row", "col"))
    plans = []
    base = 0
    for axis, own, gathered in (("row", col_ref, col_all), ("col", row_ref, row_all)):
        size, me = lax.axis_size(axis), lax.axis_index(axis)
        for d in range(1, size):
            plans.append((axis, own, gathered, lax.rem(me + d, size), lax.rem(me + size - d, size), me, base + d - 1))
        base += size - 1

    def copy_of(plan, t, arriving):
        axis, own, gathered, peer, source, me, k = plan
        return pltpu.make_async_remote_copy(
            src_ref=own.at[pl.ds(t * GROUP, GROUP)],
            dst_ref=gathered.at[t, source if arriving else me],
            send_sem=sems.at[0, k, t],
            recv_sem=sems.at[1, k, t],
            device_id={axis: peer},
            device_id_type=MESH,
        )

    @pl.loop(0, STEPS // GROUP)
    def _(t):
        for plan in plans:
            copy_of(plan, t, False).start()

    row_me, col_me = lax.axis_index("row"), lax.axis_index("col")

    @pl.loop(0, STEPS)
    def _(t):
        col_all[t // GROUP, row_me, lax.rem(t, GROUP)] = col_ref[t]
        row_all[t // GROUP, col_me, lax.rem(t, GROUP)] = row_ref[t]

    def arrive(t):
        @pl.when(lax.rem(t, GROUP) == 0)
        def _():
            for plan in plans:
                copy_of(plan, t // GROUP, True).wait_recv()

        a32[...] = row_all[t // GROUP, :, lax.rem(t, GROUP)].reshape(a32.shape).astype(jnp.float32)
        for h in range(PAIR // F2):
            b32[h] = col_all[t // GROUP, :, lax.rem(t, GROUP), :, :, h * F2 : (h + 1) * F2].reshape(b32.shape[1:]).astype(jnp.float32)
            for k in range(2 * SEGS):
                rows = b32[h, pl.ds(k, col_total, stride=2 * SEGS), :]
                b_ref[k, :, h * F2 : (h + 1) * F2] = rows.astype(jnp.bfloat16)

    def cross_rows(first, now):
        for k in range(share):
            g = first + k
            for h in range(0, PAIR, F2):
                lane = slice(h, h + F2)
                real, imag = [], []
                for s in range(SEGS):
                    ar = jnp.broadcast_to(a32[g, s : s + 1, lane], (col_total, F2)).astype(jnp.bfloat16)
                    ai = jnp.broadcast_to(a32[g, SEGS + s : SEGS + s + 1, lane], (col_total, F2)).astype(jnp.bfloat16)
                    br, bi = b_ref[s, :, lane], b_ref[SEGS + s, :, lane]
                    real.append(ar * br + ai * bi)
                    imag.append(ai * br - ar * bi)
                at = pl.ds(pl.multiple_of(g * col_total, 16), col_total)
                cross[now, 0, at, lane] = tree(real)
                cross[now, 1, at, lane] = tree(imag)

    def lag_tile(i, t):
        before = lax.rem(t + 1, 2)
        part = jnp.dot(cross[before, i // (TILES // 2)], w_ref[t - 1, i], preferred_element_type=jnp.float32)
        acc[i] = acc[i] + part

    acc[...] = jnp.zeros_like(acc)
    arrive(jnp.int32(0))

    @pl.loop(0, TILES)
    def _(i):
        cross_rows(i * share, 0)

    @pl.loop(1, STEPS)
    def _(t):
        arrive(t)

        @pl.loop(0, TILES)
        def _(i):
            lag_tile(i, t)
            cross_rows(i * share, lax.rem(t, 2))

    @pl.loop(0, TILES)
    def _(i):
        lag_tile(i, STEPS)

    pairs = row_total * col_total
    place = lax.broadcasted_iota(jnp.int32, (pairs, TILE), 0) - (col_me * col_total + row_me) * CH_DEV
    same = place == 0
    for ch in range(1, CH_DEV):
        same = same | (place == ch * (col_total + 1))
    keep = jnp.where(same, 0.0, np.float32(1.0 / math.sqrt(SEGS * NF)))
    half = TILES // 2
    leaving = []

    def leave(first):
        lane = pl.ds(first, TILE)
        copy = pltpu.make_async_copy(out_ref.at[:, lane], out_hbm.at[:, lane], out_sem.at[first // TILE])
        copy.start()
        leaving.append(copy)

    for k in range(half):
        up = (acc[k] + acc[half + k]) * keep
        down = (acc[k] - acc[half + k]) * keep
        out_ref[:, HALF + k * TILE : HALF + (k + 1) * TILE] = up.astype(jnp.bfloat16)
        leave(HALF + k * TILE)
        turned = jnp.dot(down.astype(jnp.bfloat16), flip_ref[...], preferred_element_type=jnp.float32)
        out_ref[:, HALF - (k + 1) * TILE : HALF - k * TILE] = turned.astype(jnp.bfloat16)
        leave(HALF - (k + 1) * TILE)
    for copy in leaving:
        copy.wait()

    @pl.loop(0, STEPS // GROUP)
    def _(t):
        for plan in plans:
            copy_of(plan, t, False).wait_send()


def correlate(row_own, col_own, tables):
    row_count, col_count = lax.axis_size("row"), lax.axis_size("col")
    row_total, col_total = col_count * CH_DEV, row_count * CH_DEV
    pairs = row_total * col_total
    flip = np.eye(TILE, dtype=np.float32)[::-1]
    own = row_own.shape[1:]
    return pl.pallas_call(
        correlate_kernel,
        in_specs=[pl.BlockSpec(memory_space=pltpu.VMEM)] * 4,
        out_specs=pl.BlockSpec(memory_space=pl.ANY),
        out_shape=jax.ShapeDtypeStruct((pairs, LAGS), jnp.bfloat16),
        scratch_shapes=[
            pltpu.VMEM((STEPS // GROUP, col_count, GROUP) + own, jnp.bfloat16),
            pltpu.VMEM((STEPS // GROUP, row_count, GROUP) + own, jnp.bfloat16),
            pltpu.VMEM((row_total, 2 * SEGS, PAIR), jnp.float32),
            pltpu.VMEM((PAIR // F2, col_total * 2 * SEGS, F2), jnp.float32),
            pltpu.VMEM((2 * SEGS, col_total, PAIR), jnp.bfloat16),
            pltpu.VMEM((2, 2, pairs, PAIR), jnp.bfloat16),
            pltpu.VMEM((TILES, pairs, TILE), jnp.float32),
            pltpu.VMEM((pairs, LAGS), jnp.bfloat16),
            pltpu.SemaphoreType.DMA((2, row_count + col_count - 2, STEPS // GROUP)),
            pltpu.SemaphoreType.DMA((LAGS // TILE,)),
        ],
        compiler_params=pltpu.CompilerParams(
            vmem_limit_bytes=58 << 20, collective_id=1, has_side_effects=True
        ),
    )(row_own, col_own, tables, jnp.asarray(flip, jnp.bfloat16))


def local(strain, file_channels, file_counts, window_start):
    row_count = lax.axis_size("row")
    col_count = lax.axis_size("col")
    my_row = lax.axis_index("row")
    my_col = lax.axis_index("col")
    slot_total = strain.shape[0]
    window = lax.dynamic_slice_in_dim(strain, window_start[0], SEGS * NT, 1)
    slot_index = jnp.arange(slot_total, dtype=jnp.int32)
    live_slot = slot_index < file_counts[0]
    owner_row = file_channels // CH_DEV // col_count
    local_slot = file_channels % CH_DEV
    same_owner = (owner_row[:, None] == owner_row[None, :]) & live_slot[None, :]
    earlier = slot_index[None, :] < slot_index[:, None]
    position = jnp.sum((same_owner & earlier).astype(jnp.int32), axis=1)
    target = owner_row * CAP + position
    routing = (
        jnp.arange(row_count * CAP, dtype=jnp.int32)[:, None] == target[None, :]
    ) & live_slot[None, :]
    outgoing = jnp.dot(
        routing.astype(jnp.bfloat16), window, preferred_element_type=jnp.float32
    ).astype(jnp.bfloat16)
    labels = jnp.sum(jnp.where(routing, local_slot[None, :] + 1, 0), axis=1) - 1
    tail = jnp.broadcast_to(
        labels.astype(jnp.bfloat16)[:, None, None], (row_count * CAP, SEGS, 128)
    )
    outgoing = jnp.concatenate([outgoing.reshape(row_count * CAP, SEGS, NT), tail], axis=2)
    row_own, col_own, tables = spectra_of(outgoing.reshape(row_count, CAP, SEGS, NT + 128))
    row_total = CH_DEV * col_count
    col_total = CH_DEV * row_count
    lagged = correlate(row_own, col_own, tables)
    return lagged.reshape(row_total, col_total, LAGS)


def solution(mesh):
    placed = (P(("row", "col"), None), P(("row", "col")), P(("row", "col")), P(("row", "col")))
    return jax.shard_map(
        local, mesh=mesh, in_specs=placed, out_specs=P("row", "col", None), check_vma=False
    )
```

profile of v0, /device:TPU:0, one launch (start us, length us, event | category | flops | bytes accessed | tf_op | source)
XLA Modules:
  0.0 61.4 jit_solution(17002364932703996277)
XLA Ops:
  0.0 0.0 copy-start
  1.4 0.7 %and_select_fusion.1 = (s32[8]{0:T(128)S(1)}, s32[8]{0:T(128)S(1)}) fusion(s32[8]{0:T(128)} %param.12), kind=kLoop, calls=%fused_computation.12 | loop fusion | flops 280 | bytes 96 | tf_op jit(solution)/shard_map/jit(floor_divide)/jit(_where)/select_n | solution.py:386
  2.0 0.2 convert_reduce_fusion
  2.2 0.1 select_reduce_fusion
  2.4 0.1 convert_element_type.20
  2.5 0.1 broadcast_in_dim.12
  2.5 0.0 copy-done
  2.5 0.4 convolution_convert_fusion
  2.9 0.0 copy-start.1
  2.9 0.0 copy-start.4
  2.9 0.0 copy-start.5
  2.9 0.0 copy-start.6
  3.0 0.0 copy-start.7
  3.0 0.0 copy-start.8
  3.0 0.3 copy.12
  3.3 0.6 %copy-done.1 = f32[2,128,512]{2,1,0:T(8,128)S(1)} copy-done((f32[2,128,512]{2,1,0:T(8,128)S(1)}, f32[2,128,512]{2,1,0:T(8,128)}, u32[]{:S(2)}) %copy-start.1) | copy-done | bytes 524312
  4.0 0.1 copy-done.4
  4.0 0.1 copy-done.5
  4.1 0.0 copy-done.6
  4.1 0.0 copy-done.7
  4.1 0.0 copy-done.8
  4.1 17.1 %shard_map.109 = (bf16[8,4,16,256]{3,2,1,0:T(8,128)(2,1)S(1)}, bf16[8,4,16,256]{3,2,1,0:T(8,128)(2,1)S(1)}, bf16[8,4,256,256]{3,2,1,0:T(8,128)(2,1)}) custom-call(bf16[4,2,8,4224]{3,2,1,0:T(8,128)(2,1)S(1)} %pad_maximum_fusion.out_ref, f32[2,16,256]{2,1,0:T(8,128)S(1)} %copy-done.7, bf16[512,256]{1,0:T(8,128)(2,1)S(1)} %copy-done.5, ...), custom_call_target="tpu_custom_call" | custom-call | tf_op jit(solution)/shard_map/pallas_call | solution.py:198
  21.2 0.0 copy-start.2
  21.2 0.7 %copy-done.2 = bf16[8,4,16,256]{3,2,1,0:T(8,128)(2,1)} copy-done((bf16[8,4,16,256]{3,2,1,0:T(8,128)(2,1)}, bf16[8,4,16,256]{3,2,1,0:T(8,128)(2,1)S(1)}, u32[]{:S(2)}) %copy-start.2) | copy-done | bytes 262168
  21.9 0.0 copy-start.3
  21.9 0.7 %copy-done.3 = bf16[8,4,16,256]{3,2,1,0:T(8,128)(2,1)} copy-done((bf16[8,4,16,256]{3,2,1,0:T(8,128)(2,1)}, bf16[8,4,16,256]{3,2,1,0:T(8,128)(2,1)S(1)}, u32[]{:S(2)}) %copy-start.3) | copy-done | bytes 262168
  22.6 36.5 %shard_map.110 = bf16[512,1024]{1,0:T(8,128)(2,1)} custom-call(bf16[8,4,16,256]{3,2,1,0:T(8,128)(2,1)} %copy-done.2, bf16[8,4,16,256]{3,2,1,0:T(8,128)(2,1)} %copy-done.3, bf16[8,4,256,256]{3,2,1,0:T(8,128)(2,1)} %get-tuple-element.10.w_ref, bf16[256,256]{1,0:T(8,128)(2,1)} %constant.65.clone.flip_ref), custom_call_target="tpu_custom_call" | custom-call | tf_op jit(solution)/shard_map/pallas_call | solution.py:354
  59.1 2.3 %copy.16 = bf16[32,16,1024]{2,1,0:T(8,128)(2,1)} copy(bf16[32,16,1024]{2,1,0:T(8,128)(2,1)} %bitcast.10) | data formatting | bytes 2097152
  (4 shorter events, 0.1 us)
Async XLA Ops:
  0.0 2.5 %copy-start = (bf16[8,33280]{1,0:T(8,128)(2,1)S(1)}, bf16[8,33280]{1,0:T(8,128)(2,1)}, u32[]{:S(2)}) copy-start(bf16[8,33280]{1,0:T(8,128)(2,1)} %param.11) | copy-start | bytes 1597444
  2.9 1.0 %copy-start.1 = (f32[2,128,512]{2,1,0:T(8,128)S(1)}, f32[2,128,512]{2,1,0:T(8,128)}, u32[]{:S(2)}) copy-start(f32[2,128,512]{2,1,0:T(8,128)} %constant.64.clone.refs_5_) | copy-start | bytes 1572868
  2.9 1.1 %copy-start.4 = (bf16[512,256]{1,0:T(8,128)(2,1)S(1)}, bf16[512,256]{1,0:T(8,128)(2,1)}, u32[]{:S(2)}) copy-start(bf16[512,256]{1,0:T(8,128)(2,1)} %constant.61.clone.refs_2_) | copy-start | bytes 786436
  2.9 1.2 %copy-start.5 = (bf16[512,256]{1,0:T(8,128)(2,1)S(1)}, bf16[512,256]{1,0:T(8,128)(2,1)}, u32[]{:S(2)}) copy-start(bf16[512,256]{1,0:T(8,128)(2,1)} %constant.60.clone.refs_1_) | copy-start | bytes 786436
  2.9 1.2 %copy-start.6 = (f32[2,16,512]{2,1,0:T(8,128)S(1)}, f32[2,16,512]{2,1,0:T(8,128)}, u32[]{:S(2)}) copy-start(f32[2,16,512]{2,1,0:T(8,128)} %constant.63.clone.refs_4_) | copy-start | bytes 196612
  3.0 1.1 %copy-start.7 = (f32[2,16,256]{2,1,0:T(8,128)S(1)}, f32[2,16,256]{2,1,0:T(8,128)}, u32[]{:S(2)}) copy-start(f32[2,16,256]{2,1,0:T(8,128)} %constant.59.clone.refs_0_) | copy-start | bytes 98308
  3.0 1.1 %copy-start.8 = (f32[3,16,128]{2,1,0:T(8,128)S(1)}, f32[3,16,128]{2,1,0:T(8,128)}, u32[]{:S(2)}) copy-start(f32[3,16,128]{2,1,0:T(8,128)} %constant.62.clone.refs_3_) | copy-start | bytes 73732
  21.2 0.7 %copy-start.2 = (bf16[8,4,16,256]{3,2,1,0:T(8,128)(2,1)}, bf16[8,4,16,256]{3,2,1,0:T(8,128)(2,1)S(1)}, u32[]{:S(2)}) copy-start(bf16[8,4,16,256]{3,2,1,0:T(8,128)(2,1)S(1)} %get-tuple-element.8.row_ref) | copy-start | bytes 786436
  21.9 0.7 %copy-start.3 = (bf16[8,4,16,256]{3,2,1,0:T(8,128)(2,1)}, bf16[8,4,16,256]{3,2,1,0:T(8,128)(2,1)S(1)}, u32[]{:S(2)}) copy-start(bf16[8,4,16,256]{3,2,1,0:T(8,128)(2,1)S(1)} %get-tuple-element.9.col_ref) | copy-start | bytes 786436
where the time goes:
time: 61.6 us; the launch traced here: 61.4 us
  Pallas kernels  53.6 us (87%)
  local copies, waits for them, and re-layouts  4.96 us (8%)
  between operations  1.47 us (2%)
  other arithmetic  1.04 us (2%)
    pallas_call x1, Pallas kernels, correlate(): pl.pallas_call(correlate_kernel, in_specs=[pl.BlockSpec(memory_space=pltp...  36.5 us
    pallas_call x1, Pallas kernels, spectra_of(): pl.pallas_call(spectra_kernel, out_shape=(shape, shape, jax.ShapeDtypeStr...  17.1 us
    unnamed x20, local copies, waits for them, and re-layouts  4.8 us

commit v1 on v0

v1 whole, which is shorter than its diff:
```python
import functools
import math

import jax
import jax.numpy as jnp
import numpy as np
from jax import lax
from jax.experimental import pallas as pl
from jax.experimental.pallas import tpu as pltpu
from jax.sharding import PartitionSpec as P

NF = 2048
NT = 4096
LAGS = 1024
SEGS = 8
CH_DEV = 4
CAP = 2
SMOOTH = 32
EDGE = 128
N1 = 16
N2 = NT // N1
F2 = NF // N1
HALF = LAGS // 2
PARTS = 2
PSEG = SEGS // PARTS
ROWS = CH_DEV * PSEG
BLOCK = 2 * ROWS
QUADS = 4
PAIR = QUADS * F2
TURNS = NF // PAIR
STEPS = PARTS * TURNS
TILE = 256
TILES = 2 * HALF // TILE
CORES = 2
AHEAD = 4
MESH = pl.DeviceIdType.MESH


def forward_tables():
    n2 = np.arange(N2)
    f1 = np.arange(N1)
    f2 = np.arange(F2)
    angle = 2 * np.pi * (np.outer(f1, n2) % NT) / NT
    twiddle = np.stack([np.cos(angle), -np.sin(angle)]).astype(np.float32)
    angle = 2 * np.pi * (np.outer(n2, f2) % N2) / N2
    c, s = np.cos(angle), np.sin(angle)
    second = np.block([[c, -s], [s, c]]).astype(np.float32)
    high = second.astype(jnp.bfloat16)
    low = (second - high.astype(np.float32)).astype(jnp.bfloat16)
    f = f1[:, None] + N1 * f2[None, :]
    distance = np.minimum(f + 0.5, NF - f - 0.5)
    taper = np.sin(0.5 * np.pi * np.minimum(distance / EDGE, 1.0)) ** 2
    turn = np.pi * f / NT
    shape = np.stack([taper, np.cos(turn), -np.sin(turn)]).astype(np.float32)
    return twiddle, high, low, shape


def lag_tables():
    m2 = 2 * np.arange(HALF) + 1
    f1 = np.arange(N1)
    f2 = N1 * np.arange(F2)
    a = np.pi * (np.outer(f1, m2) % (2 * NT)) / NT
    b = np.pi * (np.outer(f2, m2) % (2 * NT)) / NT
    first = np.stack([np.cos(a), np.sin(a)]).astype(np.float32)
    second = np.stack([np.cos(b), np.sin(b)]).astype(np.float32)
    return first, second


def shifted(value, lanes, amount):
    rolled = pltpu.roll(value, amount % F2, 1)
    source = lanes - amount
    return jnp.where((source >= 0) & (source < F2), rolled, 0.0)


def greet(axes):
    barrier = pltpu.get_barrier_semaphore()
    count = 0
    for axis in axes:
        size, me = lax.axis_size(axis), lax.axis_index(axis)
        for d in range(1, size):
            pl.semaphore_signal(barrier, inc=1, device_id={axis: lax.rem(me + d, size)}, device_id_type=MESH)
            count += 1
    pl.semaphore_wait(barrier, count)


def tree(terms):
    while len(terms) > 1:
        terms = [terms[k] + terms[k + 1] for k in range(0, len(terms), 2)]
    return terms[0]


def combine(values, weights):
    total = None
    for v, w in zip(values, weights):
        if abs(w) < 1e-9:
            continue
        term = v if abs(w - 1) < 1e-9 else (-v if abs(w + 1) < 1e-9 else v * np.float32(w))
        total = term if total is None else total + term
    return total


def dot(a, b):
    return jnp.dot(a, b, preferred_element_type=jnp.float32)


def chosen_rows(label):
    count = label.shape[0]
    row = lax.broadcasted_iota(jnp.int32, label.shape, 0)
    lane = lax.broadcasted_iota(jnp.int32, label.shape, 1)
    hit = (label == (lane // PSEG).astype(jnp.float32)) & (lax.rem(row, PSEG) == lax.rem(lane, PSEG))
    picks = jnp.where(hit, 1.0, 0.0)
    if count < 128:
        picks = jnp.concatenate([picks, jnp.zeros((128 - count, 128), jnp.float32)], axis=0)
    return jnp.transpose(picks)[:ROWS, :count].astype(jnp.bfloat16)


def spectra_part(part, picks, got, x_ref, z_ref, tw_ref, hi_ref, lo_ref, shape_ref, put):
    x_ref[...] = dot(picks, got[part].reshape(-1, NT))
    cosines = np.cos(2 * np.pi * np.arange(N1) / N1)
    sines = np.sin(2 * np.pi * np.arange(N1) / N1)
    for h in range(0, N2, 128):
        xs = [x_ref[:, k * N2 + h : k * N2 + h + 128] for k in range(N1)]
        even = [xs[k] + xs[k + N1 // 2] for k in range(N1 // 2)]
        odd = [xs[k] - xs[k + N1 // 2] for k in range(N1 // 2)]
        for f in range(N1 // 2 + 1):
            src = even if f % 2 == 0 else odd
            re = combine(src, [cosines[f * k % N1] for k in range(N1 // 2)])
            im = combine(src, [-sines[f * k % N1] for k in range(N1 // 2)])
            for f1, sign in {f: 1.0, (N1 - f) % N1: -1.0}.items() if f not in (0, N1 // 2) else ((f, 1.0),):
                tc = tw_ref[0, f1 : f1 + 1, h : h + 128]
                ts = tw_ref[1, f1 : f1 + 1, h : h + 128]
                if im is None:
                    zr, zi = re * tc, re * ts
                else:
                    i = im if sign > 0 else -im
                    zr, zi = re * tc - i * ts, re * ts + i * tc
                z_ref[f1 * ROWS : (f1 + 1) * ROWS, h : h + 128] = zr
                z_ref[f1 * ROWS : (f1 + 1) * ROWS, N2 + h : N2 + h + 128] = zi
    z = z_ref[...]
    zh = z.astype(jnp.bfloat16)
    zl = (z - zh.astype(jnp.float32)).astype(jnp.bfloat16)
    z_ref[:, : 2 * F2] = dot(zh, hi_ref[...]) + dot(zl, hi_ref[...]) + dot(zh, lo_ref[...])
    lanes = lax.broadcasted_iota(jnp.int32, (ROWS, F2), 1)
    piece = lambda f1, c: z_ref[f1 * ROWS : (f1 + 1) * ROWS, c * F2 : (c + 1) * F2]
    power = []
    for f1 in range(N1):
        re, im = piece(f1, 0), piece(f1, 1)
        power.append(re * re + im * im)
    prefix, suffix = [power[0]], [power[-1]]
    for k in range(1, N1):
        prefix.append(prefix[-1] + power[k])
        suffix.append(suffix[-1] + power[N1 - 1 - k])
    suffix = suffix[::-1]
    total = prefix[-1]
    reach = SMOOTH // N1
    middle = total
    for k in range(1, reach):
        middle = middle + shifted(total, lanes, k) + shifted(total, lanes, -k)
    for f1 in range(N1):
        window = middle + shifted(suffix[f1], lanes, reach) + shifted(prefix[f1], lanes, -reach)
        scale = shape_ref[0, f1 : f1 + 1] * lax.rsqrt(window * (1.0 / (2 * SMOOTH + 1)) + 1e-06)
        re, im = piece(f1, 0) * scale, piece(f1, 1) * scale
        tc, ts = shape_ref[1, f1 : f1 + 1], shape_ref[2, f1 : f1 + 1]
        put(part * TURNS + f1 // QUADS, f1 % QUADS, re, im, re * tc - im * ts, re * ts + im * tc)


def pair_kernel(out_ref, lab_ref, *refs):
    sources, refs = refs[:8], refs[8:]
    result, consts, refs = refs[0], refs[1:9], refs[9:]
    tw_ref, hi_ref, lo_ref, shape_ref, first_ref, second_ref, perm_ref, flip_ref = consts
    got, glab, x_ref, z_ref, w_ref, row_all, col_all, v_ref, b32, cross, acc, down_ref = refs[:12]
    a_send, a_recv, lab_recv, z_send, z_far, z_rest, x_send, x_same, x_mate, const_sem = refs[12:]
    rows, cols = lax.axis_size("row"), lax.axis_size("col")
    row_total, col_total = cols * CH_DEV, rows * CH_DEV
    share = col_total // TILES
    row_me, col_me = lax.axis_index("row"), lax.axis_index("col")
    hops, chips = rows // 2, cols // CORES
    far = lax.rem(row_me + hops, rows)
    chip, core = col_me // CORES, lax.rem(col_me, CORES)
    mate = chip * CORES + (1 - core)
    chip_at = lambda d: lax.rem(chip + chips - d, chips) * CORES

    loads = [pltpu.make_async_copy(f, t, const_sem.at[k]) for k, (f, t) in enumerate(zip(sources, consts))]
    for load in loads[::-1]:
        load.start()
    greet(("row", "col"))

    def remote(src, dst, send, recv, peer):
        return pltpu.make_async_remote_copy(
            src_ref=src, dst_ref=dst, send_sem=send, recv_sem=recv, device_id=peer, device_id_type=MESH
        )

    def settle(ref, sem):
        pltpu.make_async_copy(ref, ref, sem).wait()

    for d in range(1, rows):
        peer = lax.rem(row_me + d, rows)
        remote(lab_ref.at[peer], glab.at[d], a_send.at[PARTS], lab_recv, {"row": peer}).start()
    for part in range(PARTS):
        for d in range(1, rows):
            peer = lax.rem(row_me + d, rows)
            remote(out_ref.at[part, peer], got.at[part, d], a_send.at[part], a_recv.at[part], {"row": peer}).start()
    glab[0] = lab_ref[row_me]
    for part in range(PARTS):
        got[part, 0] = out_ref[part, row_me]

    def z_copy(u, origin, peer, k):
        sem = z_far if k < 2 else z_rest
        return remote(col_all.at[u, origin], col_all.at[u, origin], z_send.at[k], sem.at[u], {"row": peer})

    def x_copy(u, origin, peer, k):
        sem = x_same if k == 0 else x_mate
        return remote(row_all.at[u, origin], row_all.at[u, origin], x_send.at[k], sem.at[u], {"col": peer})

    def z_plans(u):
        out = []
        for d in range(1, hops + 1):
            up, down = row_me + d, row_me - d
            k = 0 if d == hops else 2 * d
            out.append((up < rows, z_copy(u, row_me, up, k)))
            out.append((down >= 0, z_copy(u, row_me, down, k + 1)))
        return out

    def relay_plans(u):
        out = []
        for d in range(1, hops):
            up, down = row_me + d, row_me - d
            k = 2 * hops + d - 1
            out.append(((far < row_me) & (up < rows), z_copy(u, far, up, k)))
            out.append(((far > row_me) & (down >= 0), z_copy(u, far, down, k)))
        return out

    def begin_z(u):
        for valid, copy in z_plans(u):
            pl.when(valid)(copy.start)

    def begin_x(u):
        for d in range(1, chips):
            x_copy(u, col_me, chip_at(d) + core, 0).start()
        x_copy(u, col_me, mate, 1).start()

    def serve(u):
        settle(col_all.at[u, pl.ds(0, 1)], z_far.at[u])
        for valid, copy in relay_plans(u):
            pl.when(valid)(copy.start)
        settle(row_all.at[u, pl.ds(0, chips - 1)], x_same.at[u])
        for d in range(1, chips):
            x_copy(u, chip_at(d) + core, mate, 2).start()

    def arrive(u):
        settle(col_all.at[u, pl.ds(0, rows - 2)], z_rest.at[u])
        settle(row_all.at[u, pl.ds(0, chips)], x_mate.at[u])
        for q in range(0, QUADS, 2):
            sides = [row_all[u, :, q + n].reshape(-1, F2) for n in range(2)]
            turned = dot(perm_ref[...], jnp.concatenate(sides, axis=1)).astype(jnp.bfloat16)
            for n in range(2):
                for k in range(2 * PSEG):
                    v_ref[q + n, k] = turned[k * row_total : (k + 1) * row_total, n * F2 : (n + 1) * F2]
        for q in range(QUADS):
            b32[q] = col_all[u, :, q].reshape(b32.shape[1:]).astype(jnp.float32)

    def put(u, q, re, im, tr, ti):
        for c, (a, b) in enumerate(((re, tr), (im, ti))):
            at = slice(c * ROWS, (c + 1) * ROWS)
            col_all[u, row_me, q, at] = a.astype(jnp.bfloat16)
            row_all[u, col_me, q, at] = b.astype(jnp.bfloat16)

    def cross_rows(i, now):
        for jj in range(share):
            base = pl.multiple_of((i * (share // CH_DEV) + jj // CH_DEV) * BLOCK, BLOCK)
            at = base + jj % CH_DEV * PSEG
            for q in range(QUADS):
                spread = lambda r: jnp.broadcast_to(b32[q, pl.ds(at + r, 1), :], (16, F2)).astype(jnp.bfloat16)
                br = [spread(s) for s in range(PSEG)]
                bi = [spread(ROWS + s) for s in range(PSEG)]
                for g in range(0, row_total, 16):
                    real, imag = [], []
                    for s in range(PSEG):
                        ar, ai = v_ref[q, s, g : g + 16], v_ref[q, PSEG + s, g : g + 16]
                        real.append(ar * br[s] + ai * bi[s])
                        imag.append(ai * br[s] - ar * bi[s])
                    line = pl.ds(pl.multiple_of((i * share + jj) * row_total + g, 16), 16)
                    cross[now, 0, q, line] = tree(real)
                    cross[now, 1, q, line] = tree(imag)

    def lag_tile(i, u):
        before = lax.rem(u + 1, 2)
        side = [cross[before, i // (TILES // 2), q] for q in range(QUADS)]
        term = dot(jnp.concatenate(side, axis=1), w_ref[lax.rem(u - 1, TURNS), i])
        for n in range(2):
            acc[i, n] = acc[i, n] + term[:, n * F2 : (n + 1) * F2]

    for load in loads:
        load.wait()
    for k in range(HALF // TILE):
        lane = slice(k * TILE, (k + 1) * TILE)
        bc, bs = second_ref[0, :, lane], second_ref[1, :, lane]
        for f1 in range(N1):
            ac, as_ = first_ref[0, f1 : f1 + 1, lane], first_ref[1, f1 : f1 + 1, lane]
            t, at = f1 * F2 // PAIR, slice(f1 * F2 % PAIR, f1 * F2 % PAIR + F2)
            w_ref[t, k, at, :] = (ac * bc - as_ * bs).astype(jnp.bfloat16)
            w_ref[t, HALF // TILE + k, at, :] = (-(as_ * bc + ac * bs)).astype(jnp.bfloat16)
    acc[...] = jnp.zeros_like(acc)

    tables = (tw_ref, hi_ref, lo_ref, shape_ref)
    settle(glab.at[pl.ds(1, rows - 1)], lab_recv)
    settle(got.at[0, pl.ds(1, rows - 1)], a_recv.at[0])
    picks = chosen_rows(glab[...].reshape(-1, 128).astype(jnp.float32))
    spectra_part(0, picks, got, x_ref, z_ref, *tables, put)

    @pl.loop(0, TURNS)
    def _(u):
        begin_z(u)
        begin_x(u)

    serve(0)
    settle(got.at[1, pl.ds(1, rows - 1)], a_recv.at[1])
    spectra_part(1, picks, got, x_ref, z_ref, *tables, put)

    @pl.loop(TURNS, STEPS)
    def _(u):
        begin_z(u)
        begin_x(u)

    arrive(0)

    @pl.loop(0, TILES)
    def _(i):
        cross_rows(i, 0)

        @pl.when(i == 1)
        def _():
            serve(1)

    @pl.loop(1, STEPS)
    def _(u):
        arrive(u)

        @pl.loop(0, TILES)
        def _(i):
            lag_tile(i, u)
            cross_rows(i, lax.rem(u, 2))

            @pl.when((i == 1) & (u + 1 < STEPS))
            def _():
                serve(u + 1)

    @pl.loop(0, TILES)
    def _(i):
        lag_tile(i, STEPS)

    half = TILES // 2
    place = lax.broadcasted_iota(jnp.int32, (col_total, F2), 0)
    scale = np.float32(1.0 / math.sqrt(SEGS * NF))

    @pl.loop(0, row_total)
    def _(g):
        own = g - col_me * CH_DEV
        mine = (place == row_me * CH_DEV + own) & (own >= 0) & (own < CH_DEV)
        keep = jnp.where(mine, 0.0, scale)
        for k in range(half):
            for n in range(2):
                a = acc[k, n, pl.ds(g, col_total, stride=row_total), :]
                b = acc[half + k, n, pl.ds(g, col_total, stride=row_total), :]
                first = HALF + k * TILE + n * F2
                result[g, :, first : first + F2] = ((a + b) * keep).astype(jnp.bfloat16)
                down_ref[k, n, pl.ds(pl.multiple_of(g * col_total, 16), col_total), :] = ((a - b) * keep).astype(jnp.bfloat16)

    for k in range(half):
        side = jnp.concatenate([down_ref[k, n] for n in range(2)], axis=1)
        turned = dot(side, flip_ref[...]).astype(jnp.bfloat16)
        result[:, :, HALF - (k + 1) * TILE : HALF - k * TILE] = turned.reshape(row_total, col_total, TILE)

    settle(glab.at[pl.ds(1, rows - 1)], a_send.at[PARTS])
    for part in range(PARTS):
        settle(got.at[part, pl.ds(1, rows - 1)], a_send.at[part])
    for d in range(1, hops + 1):
        k = 0 if d == hops else 2 * d
        pl.when(row_me + d < rows)(lambda k=k: settle(col_all.at[:, 0], z_send.at[k]))
        pl.when(row_me - d >= 0)(lambda k=k: settle(col_all.at[:, 0], z_send.at[k + 1]))
    for d in range(1, hops):
        k = 2 * hops + d - 1
        valid = ((far < row_me) & (row_me + d < rows)) | ((far > row_me) & (row_me - d >= 0))
        pl.when(valid)(lambda k=k: settle(col_all.at[:, 0], z_send.at[k]))
    settle(row_all.at[:, pl.ds(0, chips - 1)], x_send.at[0])
    settle(row_all.at[:, 0], x_send.at[1])
    settle(row_all.at[:, pl.ds(0, chips - 1)], x_send.at[2])


def order_table(row_total):
    table = np.zeros((2 * PSEG * row_total, 2 * PSEG * row_total), np.float32)
    for c in range(2):
        for s in range(PSEG):
            for g in range(row_total):
                at = g // CH_DEV * BLOCK + c * ROWS + g % CH_DEV * PSEG + s
                table[(c * PSEG + s) * row_total + g, at] = 1.0
    return table.astype(jnp.bfloat16)


def pairs_of(outgoing, labels):
    rows, cols = lax.axis_size("row"), lax.axis_size("col")
    row_total, col_total = cols * CH_DEV, rows * CH_DEV
    pairs = row_total * col_total
    flip = np.eye(TILE, dtype=np.float32)[::-1].astype(jnp.bfloat16)
    tables = forward_tables() + lag_tables() + (order_table(row_total), flip)
    consts = [jnp.asarray(t) for t in tables]
    block = (QUADS, BLOCK, F2)
    return pl.pallas_call(
        pair_kernel,
        out_shape=jax.ShapeDtypeStruct((row_total, col_total, LAGS), jnp.bfloat16),
        in_specs=[pl.BlockSpec(memory_space=pltpu.VMEM)] * 2 + [pl.BlockSpec(memory_space=pltpu.HBM)] * len(consts),
        out_specs=pl.BlockSpec(memory_space=pltpu.VMEM),
        scratch_shapes=[pltpu.VMEM(t.shape, t.dtype) for t in consts]
        + [
            pltpu.VMEM(outgoing.shape, jnp.bfloat16),
            pltpu.VMEM(labels.shape, jnp.bfloat16),
            pltpu.VMEM((ROWS, NT), jnp.float32),
            pltpu.VMEM((N1 * ROWS, 2 * N2), jnp.float32),
            pltpu.VMEM((TURNS, TILES, PAIR, TILE), jnp.bfloat16),
            pltpu.VMEM((STEPS, cols) + block, jnp.bfloat16),
            pltpu.VMEM((STEPS, rows) + block, jnp.bfloat16),
            pltpu.VMEM((QUADS, 2 * PSEG, row_total, F2), jnp.bfloat16),
            pltpu.VMEM((QUADS, rows * BLOCK, F2), jnp.float32),
            pltpu.VMEM((2, 2, QUADS, pairs, F2), jnp.bfloat16),
            pltpu.VMEM((TILES, 2, pairs, F2), jnp.float32),
            pltpu.VMEM((TILES // 2, 2, pairs, F2), jnp.bfloat16),
            pltpu.SemaphoreType.DMA((PARTS + 1,)),
            pltpu.SemaphoreType.DMA((PARTS,)),
            pltpu.SemaphoreType.DMA,
            pltpu.SemaphoreType.DMA((3 * (rows // 2),)),
            pltpu.SemaphoreType.DMA((STEPS,)),
            pltpu.SemaphoreType.DMA((STEPS,)),
            pltpu.SemaphoreType.DMA((3,)),
            pltpu.SemaphoreType.DMA((STEPS,)),
            pltpu.SemaphoreType.DMA((STEPS,)),
            pltpu.SemaphoreType.DMA((len(consts),)),
        ],
        compiler_params=pltpu.CompilerParams(
            vmem_limit_bytes=44 << 20, collective_id=0, has_side_effects=True
        ),
    )(outgoing, labels, *consts)


def local(strain, file_channels, file_counts, window_start):
    row_count = lax.axis_size("row")
    col_count = lax.axis_size("col")
    my_row = lax.axis_index("row")
    my_col = lax.axis_index("col")
    slot_total = strain.shape[0]
    window = lax.dynamic_slice_in_dim(strain, window_start[0], SEGS * NT, 1)
    slot_index = jnp.arange(slot_total, dtype=jnp.int32)
    live_slot = slot_index < file_counts[0]
    owner_row = file_channels // CH_DEV // col_count
    local_slot = file_channels % CH_DEV
    same_owner = (owner_row[:, None] == owner_row[None, :]) & live_slot[None, :]
    earlier = slot_index[None, :] < slot_index[:, None]
    position = jnp.sum((same_owner & earlier).astype(jnp.int32), axis=1)
    target = owner_row * CAP + position
    routing = (
        jnp.arange(row_count * CAP, dtype=jnp.int32)[:, None] == target[None, :]
    ) & live_slot[None, :]
    outgoing = jnp.dot(
        routing.astype(jnp.bfloat16), window, preferred_element_type=jnp.float32
    ).astype(jnp.bfloat16)
    labels = jnp.sum(jnp.where(routing, local_slot[None, :] + 1, 0), axis=1) - 1
    outgoing = outgoing.reshape(row_count, CAP, PARTS, PSEG, NT).transpose(2, 0, 1, 3, 4)
    labels = jnp.broadcast_to(labels.astype(jnp.bfloat16)[:, None, None], (row_count * CAP, PSEG, 128))
    return pairs_of(
        outgoing.reshape(PARTS, row_count, CAP * PSEG, NT), labels.reshape(row_count, CAP * PSEG, 128)
    )


def solution(mesh):
    placed = (P(("row", "col"), None), P(("row", "col")), P(("row", "col")), P(("row", "col")))
    return jax.shard_map(
        local, mesh=mesh, in_specs=placed, out_specs=P("row", "col", None), check_vma=False
    )
```

time: 61.6 us -> 55.1 us (0.89)
  Pallas kernels: 53.6 us -> 49 us
  local copies, waits for them, and re-layouts: 4.96 us -> 3.75 us
  other arithmetic: 1.04 us -> 0.34 us
    pallas_call x2 -> x1, Pallas kernels: 53.6 us -> 49 us  [pairs_of(): pl.pallas_call(pair_kernel, out_shape=jax.ShapeDtypeStruct((row_total, co...]
    unnamed x20 -> x21, local copies, waits for them, and re-layouts: 4.8 us -> 2.72 us
    reshape x0 -> x3, local copies, waits for them, and re-layouts: none -> 0.71 us  [the longest x2 0.59 us: local(): outgoing.reshape(row_count, CAP, PARTS, PSEG, NT).transpose(2, 0, 1, 3, 4)]
    select_n x1 -> x0, other arithmetic: 0.67 us -> none  [local(): owner_row = file_channels // CH_DEV // col_count]
where the time goes in v1:
time: 55.1 us; the launch traced here: 54.9 us
  Pallas kernels  49 us (89%)
  local copies, waits for them, and re-layouts  3.75 us (7%)
  between operations  1.48 us (3%)
    pallas_call x1, Pallas kernels, pairs_of(): pl.pallas_call(pair_kernel, out_shape=jax.ShapeDtypeStruct((row_total, co...  49 us
    unnamed x21, local copies, waits for them, and re-layouts  2.72 us

profile of v1, /device:TPU:0, one launch (start us, length us, event | category | flops | bytes accessed | tf_op | source)
XLA Modules:
  0.0 54.9 jit_solution(13590131538594209136)
XLA Ops:
  0.0 0.0 copy-start
  1.4 0.0 copy-start.9
  1.4 0.6 %copy-done.9 = s32[8]{0:T(128)S(1)} copy-done((s32[8]{0:T(128)S(1)}, s32[8]{0:T(128)}, u32[]{:S(2)}) %copy-start.9) | copy-done | bytes 56
  2.0 0.2 convert_reduce_fusion
  2.2 0.1 select_reduce_fusion
  2.4 0.1 convert_element_type.21
  2.4 0.1 broadcast_in_dim.20
  2.5 0.1 broadcast_in_dim.34
  2.6 0.1 broadcast_in_dim.35.lab_ref
  2.7 0.0 copy-done
  2.7 0.4 convolution_convert_fusion
  3.1 0.4 reshape.27
  3.5 0.0 copy-start.4
  3.5 0.0 copy-start.5
  3.5 0.0 copy-start.6
  3.5 0.0 copy-start.7
  3.5 0.0 copy-start.8
  3.5 0.2 copy.17
  3.7 0.0 copy-start.1
  3.7 0.0 copy-start.2
  3.7 0.0 copy-start.3
  3.8 0.1 reshape.28.out_ref
  3.9 0.5 copy-done.4
  4.4 0.1 copy-done.5
  4.4 0.0 copy-done.6
  4.4 0.0 copy-done.7
  4.4 0.0 copy-done.8
  4.4 0.4 copy-done.1
  4.8 0.1 copy-done.2
  4.9 0.1 copy-done.3
  5.0 49.0 %shard_map.118 = bf16[32,16,1024]{2,1,0:T(8,128)(2,1)S(1)} custom-call(bf16[2,4,8,4096]{3,2,1,0:T(8,128)(2,1)S(1)} %reshape.28.out_ref, bf16[4,8,128]{2,1,0:T(8,128)(2,1)S(1)} %broadcast_in_dim.35.lab_ref, f32[2,16,256]{2,1,0:T(8,128)S(1)} %copy-done.7, bf16[512,256]{1,0:T(8,128)(2,1)S(1)} %copy-done.3, bf16[512,256]{1,0:T(8,128)(2,1)S(1)} %copy-done.2, ...), custom_call_target="tpu_custom_call" | custom-call | tf_op jit(solution)/shard_map/pallas_call | solution.py:408
  54.0 1.0 %copy.21 = bf16[32,16,1024]{2,1,0:T(8,128)(2,1)} copy(bf16[32,16,1024]{2,1,0:T(8,128)(2,1)S(1)} %shard_map.118) | data formatting | bytes 2097152
  (4 shorter events, 0.0 us)
Async XLA Ops:
  0.0 2.7 %copy-start = (bf16[8,33280]{1,0:T(8,128)(2,1)S(1)}, bf16[8,33280]{1,0:T(8,128)(2,1)}, u32[]{:S(2)}) copy-start(bf16[8,33280]{1,0:T(8,128)(2,1)} %param.12) | copy-start | bytes 1597444
  1.4 0.7 %copy-start.9 = (s32[8]{0:T(128)S(1)}, s32[8]{0:T(128)}, u32[]{:S(2)}) copy-start(s32[8]{0:T(128)} %param.13) | copy-start | bytes 100
  3.5 0.9 %copy-start.4 = (bf16[256,256]{1,0:T(8,128)(2,1)S(1)}, bf16[256,256]{1,0:T(8,128)(2,1)}, u32[]{:S(2)}) copy-start(bf16[256,256]{1,0:T(8,128)(2,1)} %constant.68.clone.refs_7_) | copy-start | bytes 393220
  3.5 1.0 %copy-start.5 = (bf16[256,256]{1,0:T(8,128)(2,1)S(1)}, bf16[256,256]{1,0:T(8,128)(2,1)}, u32[]{:S(2)}) copy-start(bf16[256,256]{1,0:T(8,128)(2,1)} %constant.67.clone.refs_6_) | copy-start | bytes 393220
  3.5 1.0 %copy-start.6 = (f32[2,16,512]{2,1,0:T(8,128)S(1)}, f32[2,16,512]{2,1,0:T(8,128)}, u32[]{:S(2)}) copy-start(f32[2,16,512]{2,1,0:T(8,128)} %constant.65.clone.refs_4_) | copy-start | bytes 196612
  3.5 0.9 %copy-start.7 = (f32[2,16,256]{2,1,0:T(8,128)S(1)}, f32[2,16,256]{2,1,0:T(8,128)}, u32[]{:S(2)}) copy-start(f32[2,16,256]{2,1,0:T(8,128)} %constant.61.clone.refs_0_) | copy-start | bytes 98308
  3.5 0.9 %copy-start.8 = (f32[3,16,128]{2,1,0:T(8,128)S(1)}, f32[3,16,128]{2,1,0:T(8,128)}, u32[]{:S(2)}) copy-start(f32[3,16,128]{2,1,0:T(8,128)} %constant.64.clone.refs_3_) | copy-start | bytes 73732
  3.7 1.1 %copy-start.1 = (f32[2,128,512]{2,1,0:T(8,128)S(1)}, f32[2,128,512]{2,1,0:T(8,128)}, u32[]{:S(2)}) copy-start(f32[2,128,512]{2,1,0:T(8,128)} %constant.66.clone.refs_5_) | copy-start | bytes 1572868
  3.7 1.1 %copy-start.2 = (bf16[512,256]{1,0:T(8,128)(2,1)S(1)}, bf16[512,256]{1,0:T(8,128)(2,1)}, u32[]{:S(2)}) copy-start(bf16[512,256]{1,0:T(8,128)(2,1)} %constant.63.clone.refs_2_) | copy-start | bytes 786436
  3.7 1.2 %copy-start.3 = (bf16[512,256]{1,0:T(8,128)(2,1)S(1)}, bf16[512,256]{1,0:T(8,128)(2,1)}, u32[]{:S(2)}) copy-start(bf16[512,256]{1,0:T(8,128)(2,1)} %constant.62.clone.refs_1_) | copy-start | bytes 786436

commit v2 on v1

v2 whole, which is shorter than its diff:
```python
import functools
import math

import jax
import jax.numpy as jnp
import numpy as np
from jax import lax
from jax.experimental import pallas as pl
from jax.experimental.pallas import tpu as pltpu
from jax.sharding import PartitionSpec as P

NF = 2048
NT = 4096
LAGS = 1024
SEGS = 8
CH_DEV = 4
CAP = 2
SMOOTH = 32
EDGE = 128
N1 = 16
N2 = NT // N1
F2 = NF // N1
HALF = LAGS // 2
PARTS = 2
PSEG = SEGS // PARTS
ROWS = CH_DEV * PSEG
BLOCK = 2 * ROWS
QUADS = 4
PAIR = QUADS * F2
TURNS = NF // PAIR
STEPS = PARTS * TURNS
TILE = 256
TILES = 2 * HALF // TILE
CORES = 2
LEAD = 2
MESH = pl.DeviceIdType.MESH


def wave(k, period):
    bits = period.bit_length() - 1
    k = k & (period - 1)
    quarter = (4 * k + period // 2) >> bits
    r = (4 * k - (quarter << bits)).astype(jnp.float32) * np.float32(0.5 * np.pi / period)
    r2 = r * r
    odd = r * (1 + r2 * (-1 / 6 + r2 * (1 / 120 + r2 * (-1 / 5040 + r2 * (1 / 362880)))))
    even = 1 + r2 * (-1 / 2 + r2 * (1 / 24 + r2 * (-1 / 720 + r2 * (1 / 40320))))
    swap = (quarter & 1) == 1
    c, s = jnp.where(swap, odd, even), jnp.where(swap, even, odd)
    return jnp.where(((quarter + 1) & 2) == 2, -c, c), jnp.where((quarter & 2) == 2, -s, s)


def grid(shape):
    return [lax.broadcasted_iota(jnp.int32, shape, n) for n in range(2)]


def forward_tables(tw_ref, hi_ref, lo_ref, shape_ref):
    f1, n2 = grid((N1, N2))
    c, s = wave(f1 * n2, NT)
    tw_ref[0], tw_ref[1] = c, -s
    n2, f2 = grid((N2, F2))
    c, s = wave(n2 * f2, N2)
    for block, (r, l) in ((c, (0, 0)), (-s, (0, 1)), (s, (1, 0)), (c, (1, 1))):
        high = block.astype(jnp.bfloat16)
        at = slice(r * N2, (r + 1) * N2), slice(l * F2, (l + 1) * F2)
        hi_ref[at] = high
        lo_ref[at] = (block - high.astype(jnp.float32)).astype(jnp.bfloat16)
    f1, f2 = grid((N1, F2))
    f = f1 + N1 * f2
    c, s = wave(f, 2 * NT)
    rise = wave(jnp.minimum(jnp.minimum(2 * f + 1, 2 * NF - 2 * f - 1), 2 * EDGE), 8 * EDGE)[1]
    shape_ref[0], shape_ref[1], shape_ref[2] = rise * rise, c, -s


def lag_tables(w_ref):
    for k in range(HALF // TILE):
        f2, m = grid((F2, TILE))
        bc, bs = wave(N1 * f2 * (2 * (m + k * TILE) + 1), 2 * NT)
        f1, m = grid((N1, TILE))
        fc, fs = wave(f1 * (2 * (m + k * TILE) + 1), 2 * NT)
        for f in range(N1):
            ac, as_ = fc[f : f + 1], fs[f : f + 1]
            t, at = f * F2 // PAIR, slice(f * F2 % PAIR, f * F2 % PAIR + F2)
            w_ref[t, k, at, :] = (ac * bc - as_ * bs).astype(jnp.bfloat16)
            w_ref[t, HALF // TILE + k, at, :] = (-(as_ * bc + ac * bs)).astype(jnp.bfloat16)


def order_tables(perm_ref, flip_ref, row_total):
    row, lane = grid((perm_ref.shape[0], F2))
    k, g = lax.div(row, row_total), lax.rem(row, row_total)
    c, s = lax.div(k, PSEG), lax.rem(k, PSEG)
    at = lax.div(g, CH_DEV) * BLOCK + c * ROWS + lax.rem(g, CH_DEV) * PSEG + s
    for n in range(perm_ref.shape[1] // F2):
        perm_ref[:, n * F2 : (n + 1) * F2] = jnp.where(at == lane + n * F2, 1.0, 0.0).astype(jnp.bfloat16)
    row, lane = grid((TILE, TILE))
    flip_ref[...] = jnp.where(row + lane == TILE - 1, 1.0, 0.0).astype(jnp.bfloat16)


def shifted(value, lanes, amount):
    rolled = pltpu.roll(value, amount % F2, 1)
    source = lanes - amount
    return jnp.where((source >= 0) & (source < F2), rolled, 0.0)


def greet(axes):
    barrier = pltpu.get_barrier_semaphore()
    count = 0
    for axis in axes:
        size, me = lax.axis_size(axis), lax.axis_index(axis)
        for d in range(1, size):
            pl.semaphore_signal(barrier, inc=1, device_id={axis: lax.rem(me + d, size)}, device_id_type=MESH)
            count += 1
    pl.semaphore_wait(barrier, count)


def tree(terms):
    while len(terms) > 1:
        terms = [terms[k] + terms[k + 1] for k in range(0, len(terms), 2)]
    return terms[0]


def combine(values, weights):
    total = None
    for v, w in zip(values, weights):
        if abs(w) < 1e-9:
            continue
        term = v if abs(w - 1) < 1e-9 else (-v if abs(w + 1) < 1e-9 else v * np.float32(w))
        total = term if total is None else total + term
    return total


def dot(a, b):
    return jnp.dot(a, b, preferred_element_type=jnp.float32)


def chosen_rows(label):
    count = label.shape[0]
    row = lax.broadcasted_iota(jnp.int32, label.shape, 0)
    lane = lax.broadcasted_iota(jnp.int32, label.shape, 1)
    hit = (label == (lane // PSEG).astype(jnp.float32)) & (lax.rem(row, PSEG) == lax.rem(lane, PSEG))
    picks = jnp.where(hit, 1.0, 0.0)
    if count < 128:
        picks = jnp.concatenate([picks, jnp.zeros((128 - count, 128), jnp.float32)], axis=0)
    return jnp.transpose(picks)[:ROWS, :count].astype(jnp.bfloat16)


def spectra_part(part, picks, got, x_ref, z_ref, tw_ref, hi_ref, lo_ref, shape_ref, put):
    x_ref[...] = dot(picks, got[part].reshape(-1, NT))
    cosines = np.cos(2 * np.pi * np.arange(N1) / N1)
    sines = np.sin(2 * np.pi * np.arange(N1) / N1)
    for h in range(0, N2, 128):
        xs = [x_ref[:, k * N2 + h : k * N2 + h + 128] for k in range(N1)]
        even = [xs[k] + xs[k + N1 // 2] for k in range(N1 // 2)]
        odd = [xs[k] - xs[k + N1 // 2] for k in range(N1 // 2)]
        for f in range(N1 // 2 + 1):
            src = even if f % 2 == 0 else odd
            re = combine(src, [cosines[f * k % N1] for k in range(N1 // 2)])
            im = combine(src, [-sines[f * k % N1] for k in range(N1 // 2)])
            for f1, sign in {f: 1.0, (N1 - f) % N1: -1.0}.items() if f not in (0, N1 // 2) else ((f, 1.0),):
                tc = tw_ref[0, f1 : f1 + 1, h : h + 128]
                ts = tw_ref[1, f1 : f1 + 1, h : h + 128]
                if im is None:
                    zr, zi = re * tc, re * ts
                else:
                    i = im if sign > 0 else -im
                    zr, zi = re * tc - i * ts, re * ts + i * tc
                z_ref[f1 * ROWS : (f1 + 1) * ROWS, h : h + 128] = zr
                z_ref[f1 * ROWS : (f1 + 1) * ROWS, N2 + h : N2 + h + 128] = zi
    z = z_ref[...]
    zh = z.astype(jnp.bfloat16)
    zl = (z - zh.astype(jnp.float32)).astype(jnp.bfloat16)
    z_ref[:, : 2 * F2] = dot(zh, hi_ref[...]) + dot(zl, hi_ref[...]) + dot(zh, lo_ref[...])
    lanes = lax.broadcasted_iota(jnp.int32, (ROWS, F2), 1)
    piece = lambda f1, c: z_ref[f1 * ROWS : (f1 + 1) * ROWS, c * F2 : (c + 1) * F2]
    power = []
    for f1 in range(N1):
        re, im = piece(f1, 0), piece(f1, 1)
        power.append(re * re + im * im)
    prefix, suffix = [power[0]], [power[-1]]
    for k in range(1, N1):
        prefix.append(prefix[-1] + power[k])
        suffix.append(suffix[-1] + power[N1 - 1 - k])
    suffix = suffix[::-1]
    total = prefix[-1]
    reach = SMOOTH // N1
    middle = total
    for k in range(1, reach):
        middle = middle + shifted(total, lanes, k) + shifted(total, lanes, -k)
    for f1 in range(N1):
        window = middle + shifted(suffix[f1], lanes, reach) + shifted(prefix[f1], lanes, -reach)
        scale = shape_ref[0, f1 : f1 + 1] * lax.rsqrt(window * (1.0 / (2 * SMOOTH + 1)) + 1e-06)
        re, im = piece(f1, 0) * scale, piece(f1, 1) * scale
        tc, ts = shape_ref[1, f1 : f1 + 1], shape_ref[2, f1 : f1 + 1]
        put(part * TURNS + f1 // QUADS, f1 % QUADS, re, im, re * tc - im * ts, re * ts + im * tc)


def route(chan_ref, count_ref, cols, height):
    slots = chan_ref.shape[0]
    row = lax.broadcasted_iota(jnp.int32, (height, 128), 0)
    lane = lax.broadcasted_iota(jnp.int32, (height, 128), 1)
    place = lax.div(row, PSEG)
    owners = [lax.div(chan_ref[s], CH_DEV * cols) for s in range(slots)]
    live = [s < count_ref[0] for s in range(slots)]
    picks = jnp.zeros((height, 128), jnp.float32)
    label = jnp.full((height, 128), -1.0, jnp.float32)
    for s in range(slots):
        position = jnp.int32(0)
        for e in range(s):
            position = position + jnp.where(live[e] & (owners[e] == owners[s]), 1, 0)
        target = jnp.where(live[s], owners[s] * CAP + position, -1)
        hit = place == target
        picks = jnp.where(hit & (lax.rem(lane, slots) == s), 1.0, picks)
        label = jnp.where(hit, lax.rem(chan_ref[s], CH_DEV).astype(jnp.float32), label)
    picks = jnp.where(lax.rem(row, PSEG) == lax.div(lane, slots), picks, 0.0)
    return picks[:, : PSEG * slots].astype(jnp.bfloat16), label.astype(jnp.bfloat16)


def pair_kernel(win_ref, chan_ref, count_ref, *refs):
    result, tables, refs = refs[0], refs[1:5], refs[5:]
    perm_ref, flip_ref, refs = refs[0], refs[1], refs[2:]
    out_ref, lab_ref, got, glab, x_ref, z_ref, w_ref, row_all, col_all, v_ref, b32, cross, acc, down_ref = refs[:14]
    a_send, a_recv, lab_recv, z_send, z_recv, x_send, x_same, x_mate = refs[14:]
    rows, cols = lax.axis_size("row"), lax.axis_size("col")
    row_total, col_total = cols * CH_DEV, rows * CH_DEV
    wide = CH_DEV * row_total
    row_me, col_me = lax.axis_index("row"), lax.axis_index("col")
    hops, chips = rows // 2, cols // CORES
    far = lax.rem(row_me + hops, rows)
    chip, core = col_me // CORES, lax.rem(col_me, CORES)
    mate = chip * CORES + (1 - core)
    chip_at = lambda d: lax.rem(chip + chips - d, chips) * CORES

    routing, label = route(chan_ref, count_ref, cols, rows * CAP * PSEG)
    lab_ref[...] = label.reshape(lab_ref.shape)
    for part in range(PARTS):
        window = [win_ref[:, (part * PSEG + k) * NT : (part * PSEG + k + 1) * NT] for k in range(PSEG)]
        moved = dot(routing, jnp.concatenate(window, axis=0)).astype(jnp.bfloat16)
        out_ref[part] = moved.reshape(out_ref.shape[1:])
    greet(("row", "col"))

    def remote(src, dst, send, recv, peer):
        return pltpu.make_async_remote_copy(
            src_ref=src, dst_ref=dst, send_sem=send, recv_sem=recv, device_id=peer, device_id_type=MESH
        )

    def settle(ref, sem):
        pltpu.make_async_copy(ref, ref, sem).wait()

    for d in range(1, rows):
        peer = lax.rem(row_me + d, rows)
        remote(lab_ref.at[peer], glab.at[d], a_send.at[PARTS], lab_recv, {"row": peer}).start()
    for part in range(PARTS):
        for d in range(1, rows):
            peer = lax.rem(row_me + d, rows)
            remote(out_ref.at[part, peer], got.at[part, d], a_send.at[part], a_recv.at[part], {"row": peer}).start()
    glab[0] = lab_ref[row_me]
    for part in range(PARTS):
        got[part, 0] = out_ref[part, row_me]

    last = rows - 1
    far_up, far_down = (far < row_me) & (row_me < last), (far > row_me) & (row_me > 0)
    near_up, near_down = row_me == last - 1, row_me == 1
    near = jnp.where(near_up, row_me - (hops - 1), row_me + (hops - 1))

    def z_copy(u, origin, peer, k):
        block = col_all.at[u, origin]
        return remote(block, block, z_send.at[k], z_recv.at[origin, u], {"row": peer})

    def x_copy(u, origin, peer, k):
        sem = x_same if k == 0 else x_mate
        return remote(row_all.at[u, origin], row_all.at[u, origin], x_send.at[k], sem.at[u], {"col": peer})

    def begin(u, part):
        for d in range(hops, 0, -1):
            up, down = row_me + d, row_me - d
            cut = 1 if part == PARTS - 1 and d == hops and hops > 1 else 0
            pl.when(up <= last - cut)(z_copy(u, row_me, up, 2 * d - 2).start)
            pl.when(down >= cut)(z_copy(u, row_me, down, 2 * d - 1).start)
        for d in range(1, chips):
            x_copy(u, col_me, chip_at(d) + core, 0).start()
        x_copy(u, col_me, mate, 1).start()

    def relay(u):
        settled = lambda origin: settle(col_all.at[u, pl.ds(0, 1)], z_recv.at[origin, u])
        if hops > 1:

            @pl.when((u >= TURNS * (PARTS - 1)) & (near_up | near_down))
            def _():
                settled(near)
                pl.when(near_up)(z_copy(u, near, last, 2 * hops + hops - 1).start)
                pl.when(near_down)(z_copy(u, near, 0, 2 * hops + hops - 1).start)

        @pl.when(far_up | far_down)
        def _():
            settled(far)
            for d in range(1, hops):
                k = 2 * hops + d - 1
                pl.when(far_up & (row_me + d <= last))(z_copy(u, far, row_me + d, k).start)
                pl.when(far_down & (row_me - d >= 0))(z_copy(u, far, row_me - d, k).start)

    def forward(u):
        settle(row_all.at[u, pl.ds(0, chips - 1)], x_same.at[u])
        for d in range(1, chips):
            x_copy(u, chip_at(d) + core, mate, 2).start()

    def origin_of(k):
        origin, bit = row_me, 1
        while bit < rows:
            flip = lax.rem(k // bit, 2)
            origin = origin + flip * bit * (1 - 2 * lax.rem(row_me // bit, 2))
            bit *= 2
        return origin

    def arrive(u):
        settle(row_all.at[u, pl.ds(0, chips)], x_mate.at[u])
        for q in range(0, QUADS, 2):
            sides = [row_all[u, :, q + n].reshape(-1, F2) for n in range(2)]
            turned = dot(perm_ref[...], jnp.concatenate(sides, axis=1)).astype(jnp.bfloat16)
            for n in range(2):
                for j in range(2 * PSEG):
                    v_ref[q + n, j] = turned[j * row_total : (j + 1) * row_total, n * F2 : (n + 1) * F2]

    origins = [origin_of(k) for k in range(rows)]
    relays_far, relays_near = far_up | far_down, near_up | near_down

    def meet(u, part, k, more):
        origin = origins[k]
        if k > 0:
            known = (origin == far) & relays_far
            if hops > 1 and part == PARTS - 1:
                known = known | ((origin == near) & relays_near)

            @pl.when(jnp.logical_not(known))
            def _():
                settle(col_all.at[u, pl.ds(0, 1)], z_recv.at[origin, u])

        if k == 1:
            pl.when(more)(lambda: relay(u + LEAD))
        if k == 2 % rows:
            pl.when(u + LEAD < STEPS)(lambda: forward(u + LEAD))

    def put(u, q, re, im, tr, ti):
        for c, (a, b) in enumerate(((re, tr), (im, ti))):
            at = slice(c * ROWS, (c + 1) * ROWS)
            col_all[u, row_me, q, at] = a.astype(jnp.bfloat16)
            row_all[u, col_me, q, at] = b.astype(jnp.bfloat16)

    def cross_item(u, k):
        origin, now = origins[k], lax.rem(u, TURNS)
        for q in range(QUADS):
            b32[q] = col_all[u, origin, q].astype(jnp.float32)
        for q in range(QUADS):
            for ch in range(CH_DEV):
                spread = lambda r: jnp.broadcast_to(b32[q, r : r + 1, :], (16, F2)).astype(jnp.bfloat16)
                br = [spread(ch * PSEG + s) for s in range(PSEG)]
                bi = [spread(ROWS + ch * PSEG + s) for s in range(PSEG)]
                for g in range(0, row_total, 16):
                    real, imag = [], []
                    for s in range(PSEG):
                        ar, ai = v_ref[q, s, g : g + 16], v_ref[q, PSEG + s, g : g + 16]
                        real.append(br[s] * ar + bi[s] * ai)
                        imag.append(br[s] * ai - bi[s] * ar)
                    line = pl.ds(pl.multiple_of(origin * wide + ch * row_total + g, 16), 16)
                    cross[now, 0, q, line] = tree(real)
                    cross[now, 1, q, line] = tree(imag)

    def lags(first, count, fresh, beside=None):
        @pl.loop(0, TILES)
        def _(i):
            if beside is not None:
                beside(i)
            side = [cross[first + n, i // (TILES // 2), q] for n in range(count) for q in range(QUADS)]
            table = w_ref[pl.ds(first, count), i].reshape(count * PAIR, TILE)
            term = dot(jnp.concatenate(side, axis=1), table)
            for h in range(2):
                piece = term[:, h * F2 : (h + 1) * F2]
                acc[i, h] = piece if fresh else acc[i, h] + piece

    forward_tables(*tables)
    lag_tables(w_ref)
    order_tables(perm_ref, flip_ref, row_total)
    settle(glab.at[pl.ds(1, rows - 1)], lab_recv)
    settle(got.at[0, pl.ds(1, rows - 1)], a_recv.at[0])
    picks = chosen_rows(glab[...].reshape(-1, 128).astype(jnp.float32))
    spectra_part(0, picks, got, x_ref, z_ref, *tables, put)

    @pl.loop(0, TURNS)
    def _(u):
        begin(u, 0)

    for u in range(LEAD):
        forward(u)
    settle(got.at[1, pl.ds(1, rows - 1)], a_recv.at[1])
    spectra_part(1, picks, got, x_ref, z_ref, *tables, put)

    @pl.loop(TURNS, STEPS)
    def _(u):
        begin(u, 1)

    for u in range(LEAD):
        relay(u)

    def step(u, part, more):
        arrive(u)
        for k in range(rows):
            meet(u, part, k, more)
            cross_item(u, k)

    @pl.loop(0, TURNS)
    def _(u):
        step(u, 0, u + LEAD < TURNS)

    def beside(i):
        @pl.when(lax.rem(i, TILES // LEAD) == 0)
        def _():
            relay(TURNS + i // (TILES // LEAD))

    lags(0, TURNS, True, beside)

    @pl.loop(0, TURNS // 2)
    def _(p):
        @pl.loop(0, 2)
        def _(n):
            u = TURNS + 2 * p + n
            step(u, 1, u + LEAD < STEPS)

        lags(2 * p, 2, False)

    half = TILES // 2
    place = lax.broadcasted_iota(jnp.int32, (col_total, F2), 0)
    scale = np.float32(1.0 / math.sqrt(SEGS * NF))

    @pl.loop(0, row_total)
    def _(g):
        own = g - col_me * CH_DEV
        mine = (place == row_me * CH_DEV + own) & (own >= 0) & (own < CH_DEV)
        keep = jnp.where(mine, 0.0, scale)
        for k in range(half):
            for n in range(2):
                a = acc[k, n, pl.ds(g, col_total, stride=row_total), :]
                b = acc[half + k, n, pl.ds(g, col_total, stride=row_total), :]
                first = HALF + k * TILE + n * F2
                result[g, :, first : first + F2] = ((a + b) * keep).astype(jnp.bfloat16)
                down_ref[k, n, pl.ds(pl.multiple_of(g * col_total, 16), col_total), :] = ((a - b) * keep).astype(jnp.bfloat16)

    for k in range(half):
        side = jnp.concatenate([down_ref[k, n] for n in range(2)], axis=1)
        turned = dot(side, flip_ref[...]).astype(jnp.bfloat16)
        result[:, :, HALF - (k + 1) * TILE : HALF - k * TILE] = turned.reshape(row_total, col_total, TILE)

    settle(glab.at[pl.ds(1, rows - 1)], a_send.at[PARTS])
    for part in range(PARTS):
        settle(got.at[part, pl.ds(1, rows - 1)], a_send.at[part])
    whole, short = col_all.at[:, 0], col_all.at[pl.ds(0, STEPS - TURNS), 0]
    for d in range(1, hops + 1):
        cut = 1 if d == hops and hops > 1 else 0
        up, down = row_me + d, row_me - d
        pl.when(up <= last - cut)(lambda k=2 * d - 2: settle(whole, z_send.at[k]))
        pl.when(down >= cut)(lambda k=2 * d - 1: settle(whole, z_send.at[k]))
        if cut:
            pl.when(up == last)(lambda k=2 * d - 2: settle(short, z_send.at[k]))
            pl.when(down == 0)(lambda k=2 * d - 1: settle(short, z_send.at[k]))
    for d in range(1, hops):
        sent = (far_up & (row_me + d <= last)) | (far_down & (row_me - d >= 0))
        pl.when(sent)(lambda k=2 * hops + d - 1: settle(whole, z_send.at[k]))
    if hops > 1:
        pl.when(near_up | near_down)(lambda: settle(short, z_send.at[3 * hops - 1]))
    settle(row_all.at[:, pl.ds(0, chips - 1)], x_send.at[0])
    settle(row_all.at[:, 0], x_send.at[1])
    settle(row_all.at[:, pl.ds(0, chips - 1)], x_send.at[2])


def pairs_of(window, file_channels, file_counts):
    rows, cols = lax.axis_size("row"), lax.axis_size("col")
    row_total, col_total = cols * CH_DEV, rows * CH_DEV
    pairs = row_total * col_total
    order = 2 * PSEG * row_total
    block = (QUADS, BLOCK, F2)
    return pl.pallas_call(
        pair_kernel,
        out_shape=jax.ShapeDtypeStruct((row_total, col_total, LAGS), jnp.bfloat16),
        in_specs=[pl.BlockSpec(memory_space=pltpu.VMEM)] + [pl.BlockSpec(memory_space=pltpu.SMEM)] * 2,
        out_specs=pl.BlockSpec(memory_space=pltpu.VMEM),
        scratch_shapes=[
            pltpu.VMEM((2, N1, N2), jnp.float32),
            pltpu.VMEM((2 * N2, 2 * F2), jnp.bfloat16),
            pltpu.VMEM((2 * N2, 2 * F2), jnp.bfloat16),
            pltpu.VMEM((3, N1, F2), jnp.float32),
            pltpu.VMEM((order, order), jnp.bfloat16),
            pltpu.VMEM((TILE, TILE), jnp.bfloat16),
            pltpu.VMEM((PARTS, rows, CAP * PSEG, NT), jnp.bfloat16),
            pltpu.VMEM((rows, CAP * PSEG, 128), jnp.bfloat16),
            pltpu.VMEM((PARTS, rows, CAP * PSEG, NT), jnp.bfloat16),
            pltpu.VMEM((rows, CAP * PSEG, 128), jnp.bfloat16),
            pltpu.VMEM((ROWS, NT), jnp.float32),
            pltpu.VMEM((N1 * ROWS, 2 * N2), jnp.float32),
            pltpu.VMEM((TURNS, TILES, PAIR, TILE), jnp.bfloat16),
            pltpu.VMEM((STEPS, cols) + block, jnp.bfloat16),
            pltpu.VMEM((STEPS, rows) + block, jnp.bfloat16),
            pltpu.VMEM((QUADS, 2 * PSEG, row_total, F2), jnp.bfloat16),
            pltpu.VMEM((QUADS, BLOCK, F2), jnp.float32),
            pltpu.VMEM((TURNS, 2, QUADS, pairs, F2), jnp.bfloat16),
            pltpu.VMEM((TILES, 2, pairs, F2), jnp.float32),
            pltpu.VMEM((TILES // 2, 2, pairs, F2), jnp.bfloat16),
            pltpu.SemaphoreType.DMA((PARTS + 1,)),
            pltpu.SemaphoreType.DMA((PARTS,)),
            pltpu.SemaphoreType.DMA,
            pltpu.SemaphoreType.DMA((3 * (rows // 2),)),
            pltpu.SemaphoreType.DMA((rows, STEPS)),
            pltpu.SemaphoreType.DMA((3,)),
            pltpu.SemaphoreType.DMA((STEPS,)),
            pltpu.SemaphoreType.DMA((STEPS,)),
        ],
        compiler_params=pltpu.CompilerParams(
            vmem_limit_bytes=48 << 20, collective_id=0, has_side_effects=True
        ),
    )(window, file_channels, file_counts)


def local(strain, file_channels, file_counts, window_start):
    window = lax.dynamic_slice_in_dim(strain, window_start[0], SEGS * NT, 1)
    return pairs_of(window, file_channels, file_counts)


def solution(mesh):
    placed = (P(("row", "col"), None), P(("row", "col")), P(("row", "col")), P(("row", "col")))
    return jax.shard_map(
        local, mesh=mesh, in_specs=placed, out_specs=P("row", "col", None), check_vma=False
    )
```

time: 55.1 us -> 49.7 us (0.902)
  Pallas kernels: 49 us -> 46.6 us
  local copies, waits for them, and re-layouts: 3.75 us -> 1.62 us
    pallas_call x1, Pallas kernels: 49 us -> 46.6 us  [pairs_of(): pl.pallas_call(pair_kernel, out_shape=jax.ShapeDtypeStruct((row_total, co...]
    unnamed x21 -> x5, local copies, waits for them, and re-layouts: 2.72 us -> 1.41 us
    reshape x3 -> x0, local copies, waits for them, and re-layouts: 0.71 us -> none  [the longest x2 0.59 us: local(): outgoing.reshape(row_count, CAP, PARTS, PSEG, NT).transpose(2, 0, 1, 3, 4)]
where the time goes in v2:
time: 49.7 us; the launch traced here: 49.6 us
  Pallas kernels  46.6 us (94%)
  local copies, waits for them, and re-layouts  1.62 us (3%)
  between operations  1.39 us (3%)
    pallas_call x1, Pallas kernels, pairs_of(): pl.pallas_call(pair_kernel, out_shape=jax.ShapeDtypeStruct((row_total, co...  46.6 us
    unnamed x5, local copies, waits for them, and re-layouts  1.41 us

profile of v2, /device:TPU:0, one launch (start us, length us, event | category | flops | bytes accessed | tf_op | source)
XLA Modules:
  0.0 49.6 jit_solution(8535240110432267707)
XLA Ops:
  0.0 0.0 copy-start
  1.4 0.0 copy-done
  1.4 0.0 copy-start.1
  1.4 0.2 constant_dynamic-slice_fusion.win_ref
  1.6 0.4 copy-done.1
  2.0 46.6 %shard_map.46 = bf16[32,16,1024]{2,1,0:T(8,128)(2,1)S(1)} custom-call(bf16[8,32768]{1,0:T(8,128)(2,1)S(1)} %constant_dynamic-slice_fusion.win_ref, s32[8]{0:T(128)S(1)} %copy-done.1, s32[1]{0:T(128)S(6)} %copy.6.count_ref), custom_call_target="tpu_custom_call" | custom-call | tf_op jit(solution)/shard_map/pallas_call | solution.py:478
  48.6 1.0 %copy.8 = bf16[32,16,1024]{2,1,0:T(8,128)(2,1)} copy(bf16[32,16,1024]{2,1,0:T(8,128)(2,1)S(1)} %shard_map.46) | data formatting | bytes 2097152
Async XLA Ops:
  0.0 1.4 %copy-start = (bf16[8,33280]{1,0:T(8,128)(2,1)S(1)}, bf16[8,33280]{1,0:T(8,128)(2,1)}, u32[]{:S(2)}) copy-start(bf16[8,33280]{1,0:T(8,128)(2,1)} %param.4) | copy-start | bytes 1597444
  1.4 0.7 %copy-start.1 = (s32[8]{0:T(128)S(1)}, s32[8]{0:T(128)}, u32[]{:S(2)}) copy-start(s32[8]{0:T(128)} %chan_ref.1) | copy-start | bytes 100

commit v3 on v2

--- a/solution.py
+++ b/solution.py
@@ -72,11 +72,12 @@
 
 
 def lag_tables(w_ref):
+    scale = np.float32(1.0 / math.sqrt(SEGS * NF))
     for k in range(HALF // TILE):
         f2, m = grid((F2, TILE))
         bc, bs = wave(N1 * f2 * (2 * (m + k * TILE) + 1), 2 * NT)
         f1, m = grid((N1, TILE))
-        fc, fs = wave(f1 * (2 * (m + k * TILE) + 1), 2 * NT)
+        fc, fs = [v * scale for v in wave(f1 * (2 * (m + k * TILE) + 1), 2 * NT)]
         for f in range(N1):
             ac, as_ = fc[f : f + 1], fs[f : f + 1]
             t, at = f * F2 // PAIR, slice(f * F2 % PAIR, f * F2 % PAIR + F2)
@@ -334,9 +335,11 @@
                 settle(col_all.at[u, pl.ds(0, 1)], z_recv.at[origin, u])
 
         if k == 1:
-            pl.when(more)(lambda: relay(u + LEAD))
+            if more is not False:
+                pl.when(more)(lambda: relay(u + LEAD))
         if k == 2 % rows:
-            pl.when(u + LEAD < STEPS)(lambda: forward(u + LEAD))
+            if more is not False:
+                pl.when(u + LEAD < STEPS)(lambda: forward(u + LEAD))
 
     def put(u, q, re, im, tr, ti):
         for c, (a, b) in enumerate(((re, tr), (im, ti))):
@@ -364,8 +367,7 @@
                     cross[now, 1, q, line] = tree(imag)
 
     def lags(first, count, fresh, beside=None):
-        @pl.loop(0, TILES)
-        def _(i):
+        for i in range(TILES):
             if beside is not None:
                 beside(i)
             side = [cross[first + n, i // (TILES // 2), q] for n in range(count) for q in range(QUADS)]
@@ -410,42 +412,41 @@
         step(u, 0, u + LEAD < TURNS)
 
     def beside(i):
-        @pl.when(lax.rem(i, TILES // LEAD) == 0)
-        def _():
+        if i % (TILES // LEAD) == 0:
             relay(TURNS + i // (TILES // LEAD))
 
     lags(0, TURNS, True, beside)
 
-    @pl.loop(0, TURNS // 2)
-    def _(p):
-        @pl.loop(0, 2)
-        def _(n):
-            u = TURNS + 2 * p + n
-            step(u, 1, u + LEAD < STEPS)
-
-        lags(2 * p, 2, False)
+    @pl.loop(TURNS, STEPS - 1)
+    def _(u):
+        step(u, 1, u + LEAD < STEPS)
+
+    lags(0, TURNS - 1, False)
+    step(STEPS - 1, 1, False)
+    lags(TURNS - 1, 1, False)
 
     half = TILES // 2
-    place = lax.broadcasted_iota(jnp.int32, (col_total, F2), 0)
-    scale = np.float32(1.0 / math.sqrt(SEGS * NF))
-
-    @pl.loop(0, row_total)
-    def _(g):
-        own = g - col_me * CH_DEV
-        mine = (place == row_me * CH_DEV + own) & (own >= 0) & (own < CH_DEV)
-        keep = jnp.where(mine, 0.0, scale)
-        for k in range(half):
+    blank = jnp.zeros((1, F2), jnp.float32)
+    for ch in range(CH_DEV):
+        line = pl.ds(row_me * wide + ch * row_total + col_me * CH_DEV + ch, 1)
+        for i in range(TILES):
             for n in range(2):
-                a = acc[k, n, pl.ds(g, col_total, stride=row_total), :]
-                b = acc[half + k, n, pl.ds(g, col_total, stride=row_total), :]
+                acc[i, n, line] = blank
+
+    for k in range(half):
+        @pl.loop(0, col_total)
+        def _(j):
+            line = pl.ds(pl.multiple_of(j * row_total, 16), row_total)
+            for n in range(2):
+                a, b = acc[k, n, line, :], acc[half + k, n, line, :]
                 first = HALF + k * TILE + n * F2
-                result[g, :, first : first + F2] = ((a + b) * keep).astype(jnp.bfloat16)
-                down_ref[k, n, pl.ds(pl.multiple_of(g * col_total, 16), col_total), :] = ((a - b) * keep).astype(jnp.bfloat16)
+                result[j, :, first : first + F2] = (a + b).astype(jnp.bfloat16)
+                down_ref[k, n, line, :] = (a - b).astype(jnp.bfloat16)
 
     for k in range(half):
         side = jnp.concatenate([down_ref[k, n] for n in range(2)], axis=1)
         turned = dot(side, flip_ref[...]).astype(jnp.bfloat16)
-        result[:, :, HALF - (k + 1) * TILE : HALF - k * TILE] = turned.reshape(row_total, col_total, TILE)
+        result[:, :, HALF - (k + 1) * TILE : HALF - k * TILE] = turned.reshape(col_total, row_total, TILE)
 
     settle(glab.at[pl.ds(1, rows - 1)], a_send.at[PARTS])
     for part in range(PARTS):
@@ -477,7 +478,7 @@
     block = (QUADS, BLOCK, F2)
     return pl.pallas_call(
         pair_kernel,
-        out_shape=jax.ShapeDtypeStruct((row_total, col_total, LAGS), jnp.bfloat16),
+        out_shape=jax.ShapeDtypeStruct((col_total, row_total, LAGS), jnp.bfloat16),
         in_specs=[pl.BlockSpec(memory_space=pltpu.VMEM)] + [pl.BlockSpec(memory_space=pltpu.SMEM)] * 2,
         out_specs=pl.BlockSpec(memory_space=pltpu.VMEM),
         scratch_shapes=[
@@ -518,7 +519,7 @@
 
 def local(strain, file_channels, file_counts, window_start):
     window = lax.dynamic_slice_in_dim(strain, window_start[0], SEGS * NT, 1)
-    return pairs_of(window, file_channels, file_counts)
+    return jnp.transpose(pairs_of(window, file_channels, file_counts), (1, 0, 2))
 
 
 def solution(mesh):

time: 49.7 us -> 47 us (0.946)
  Pallas kernels: 46.6 us -> 43.2 us
  local copies, waits for them, and re-layouts: 1.62 us -> 2.19 us
    pallas_call x1, Pallas kernels: 46.6 us -> 43.2 us  [pairs_of(): pl.pallas_call(pair_kernel, out_shape=jax.ShapeDtypeStruct((col_total, ro...]
    transpose x0 -> x1, local copies, waits for them, and re-layouts: none -> 1.55 us  [local(): jnp.transpose(pairs_of(window, file_channels, file_counts), (1, 0, 2))]
    unnamed x5 -> x4, local copies, waits for them, and re-layouts: 1.41 us -> 0.43 us
where the time goes in v3:
time: 47 us; the launch traced here: 46.8 us
  Pallas kernels  43.2 us (92%)
  local copies, waits for them, and re-layouts  2.19 us (5%)
  between operations  1.39 us (3%)
    pallas_call x1, Pallas kernels, pairs_of(): pl.pallas_call(pair_kernel, out_shape=jax.ShapeDtypeStruct((col_total, ro...  43.2 us
    transpose x1, local copies, waits for them, and re-layouts, local(): jnp.transpose(pairs_of(window, file_channels, file_counts), (1, 0, 2))  1.55 us

profile of v3, /device:TPU:0, one launch (start us, length us, event | category | flops | bytes accessed | tf_op | source)
XLA Modules:
  0.0 46.8 jit_solution(8969958136197212022)
XLA Ops:
  0.0 0.0 copy-start
  1.4 0.0 copy-done
  1.4 0.0 copy-start.1
  1.4 0.2 constant_dynamic-slice_fusion.win_ref
  1.6 0.4 copy-done.1
  2.0 43.2 %shard_map.46 = bf16[16,32,1024]{2,1,0:T(8,128)(2,1)S(1)} custom-call(bf16[8,32768]{1,0:T(8,128)(2,1)S(1)} %constant_dynamic-slice_fusion.win_ref, s32[8]{0:T(128)S(1)} %copy-done.1, s32[1]{0:T(128)S(6)} %copy.6.count_ref), custom_call_target="tpu_custom_call" | custom-call | tf_op jit(solution)/shard_map/pallas_call | solution.py:479
  45.3 1.5 %copy.5 = bf16[32,16,1024]{2,1,0:T(8,128)(2,1)} copy(bf16[32,16,1024]{2,0,1:T(8,128)(2,1)S(1)} %bitcast.5) | data formatting | bytes 2097152 | tf_op jit(solution)/shard_map/transpose | solution.py:522
Async XLA Ops:
  0.0 1.4 %copy-start = (bf16[8,33280]{1,0:T(8,128)(2,1)S(1)}, bf16[8,33280]{1,0:T(8,128)(2,1)}, u32[]{:S(2)}) copy-start(bf16[8,33280]{1,0:T(8,128)(2,1)} %param.4) | copy-start | bytes 1597444
  1.4 0.7 %copy-start.1 = (s32[8]{0:T(128)S(1)}, s32[8]{0:T(128)}, u32[]{:S(2)}) copy-start(s32[8]{0:T(128)} %chan_ref.1) | copy-start | bytes 100

commit v4 on v3

--- a/solution.py
+++ b/solution.py
@@ -103,14 +103,14 @@
 
 
 def greet(axes):
+    count = 0
     barrier = pltpu.get_barrier_semaphore()
-    count = 0
     for axis in axes:
         size, me = lax.axis_size(axis), lax.axis_index(axis)
         for d in range(1, size):
             pl.semaphore_signal(barrier, inc=1, device_id={axis: lax.rem(me + d, size)}, device_id_type=MESH)
             count += 1
-    pl.semaphore_wait(barrier, count)
+    return lambda: pl.semaphore_wait(barrier, count)
 
 
 def tree(terms):
@@ -215,11 +215,11 @@
     return picks[:, : PSEG * slots].astype(jnp.bfloat16), label.astype(jnp.bfloat16)
 
 
-def pair_kernel(win_ref, chan_ref, count_ref, *refs):
+def pair_kernel(win_ref, chan_hbm, count_hbm, *refs):
     result, tables, refs = refs[0], refs[1:5], refs[5:]
     perm_ref, flip_ref, refs = refs[0], refs[1], refs[2:]
     out_ref, lab_ref, got, glab, x_ref, z_ref, w_ref, row_all, col_all, v_ref, b32, cross, acc, down_ref = refs[:14]
-    a_send, a_recv, lab_recv, z_send, z_recv, x_send, x_same, x_mate = refs[14:]
+    a_send, a_recv, lab_recv, z_send, z_recv, x_send, x_same, x_mate, chan_ref, count_ref, fetch_sem = refs[14:]
     rows, cols = lax.axis_size("row"), lax.axis_size("col")
     row_total, col_total = cols * CH_DEV, rows * CH_DEV
     wide = CH_DEV * row_total
@@ -230,13 +230,19 @@
     mate = chip * CORES + (1 - core)
     chip_at = lambda d: lax.rem(chip + chips - d, chips) * CORES
 
+    fetches = [pltpu.make_async_copy(f, t, fetch_sem.at[n]) for n, (f, t) in enumerate(((chan_hbm, chan_ref), (count_hbm, count_ref)))]
+    for fetch in fetches:
+        fetch.start()
+    met = greet(("row", "col"))
+    for fetch in fetches:
+        fetch.wait()
     routing, label = route(chan_ref, count_ref, cols, rows * CAP * PSEG)
     lab_ref[...] = label.reshape(lab_ref.shape)
     for part in range(PARTS):
         window = [win_ref[:, (part * PSEG + k) * NT : (part * PSEG + k + 1) * NT] for k in range(PSEG)]
         moved = dot(routing, jnp.concatenate(window, axis=0)).astype(jnp.bfloat16)
         out_ref[part] = moved.reshape(out_ref.shape[1:])
-    greet(("row", "col"))
+    met()
 
     def remote(src, dst, send, recv, peer):
         return pltpu.make_async_remote_copy(
@@ -479,7 +485,7 @@
     return pl.pallas_call(
         pair_kernel,
         out_shape=jax.ShapeDtypeStruct((col_total, row_total, LAGS), jnp.bfloat16),
-        in_specs=[pl.BlockSpec(memory_space=pltpu.VMEM)] + [pl.BlockSpec(memory_space=pltpu.SMEM)] * 2,
+        in_specs=[pl.BlockSpec(memory_space=pltpu.VMEM)] + [pl.BlockSpec(memory_space=pltpu.HBM)] * 2,
         out_specs=pl.BlockSpec(memory_space=pltpu.VMEM),
         scratch_shapes=[
             pltpu.VMEM((2, N1, N2), jnp.float32),
@@ -510,6 +516,9 @@
             pltpu.SemaphoreType.DMA((3,)),
             pltpu.SemaphoreType.DMA((STEPS,)),
             pltpu.SemaphoreType.DMA((STEPS,)),
+            pltpu.SMEM(file_channels.shape, jnp.int32),
+            pltpu.SMEM(file_counts.shape, jnp.int32),
+            pltpu.SemaphoreType.DMA((2,)),
         ],
         compiler_params=pltpu.CompilerParams(
             vmem_limit_bytes=48 << 20, collective_id=0, has_side_effects=True

time: 47 us -> 46.1 us (0.981)
  Pallas kernels: 43.2 us -> 42.3 us
    pallas_call x1, Pallas kernels: 43.2 us -> 42.3 us  [pairs_of(): pl.pallas_call(pair_kernel, out_shape=jax.ShapeDtypeStruct((col_total, ro...]
where the time goes in v4:
time: 46.1 us; the launch traced here: 45.9 us
  Pallas kernels  42.3 us (92%)
  local copies, waits for them, and re-layouts  2.19 us (5%)
  between operations  1.39 us (3%)
    pallas_call x1, Pallas kernels, pairs_of(): pl.pallas_call(pair_kernel, out_shape=jax.ShapeDtypeStruct((col_total, ro...  42.3 us
    transpose x1, local copies, waits for them, and re-layouts, local(): jnp.transpose(pairs_of(window, file_channels, file_counts), (1, 0, 2))  1.55 us

profile of v4, /device:TPU:0, one launch (start us, length us, event | category | flops | bytes accessed | tf_op | source)
XLA Modules:
  0.0 45.9 jit_solution(3188711435385741864)
XLA Ops:
  0.0 0.0 copy-start
  1.4 0.0 copy-done
  1.4 0.0 copy-start.1
  1.4 0.2 constant_dynamic-slice_fusion.win_ref
  1.6 0.4 copy-done.1
  2.0 42.3 %shard_map.46 = bf16[16,32,1024]{2,1,0:T(8,128)(2,1)S(1)} custom-call(bf16[8,32768]{1,0:T(8,128)(2,1)S(1)} %constant_dynamic-slice_fusion.win_ref, s32[8]{0:T(128)S(1)} %copy-done.1, s32[1]{0:T(128)S(6)} %copy.6.count_hbm), custom_call_target="tpu_custom_call" | custom-call | tf_op jit(solution)/shard_map/pallas_call | solution.py:485
  44.4 1.5 %copy.5 = bf16[32,16,1024]{2,1,0:T(8,128)(2,1)} copy(bf16[32,16,1024]{2,0,1:T(8,128)(2,1)S(1)} %bitcast.5) | data formatting | bytes 2097152 | tf_op jit(solution)/shard_map/transpose | solution.py:531
Async XLA Ops:
  0.0 1.4 %copy-start = (bf16[8,33280]{1,0:T(8,128)(2,1)S(1)}, bf16[8,33280]{1,0:T(8,128)(2,1)}, u32[]{:S(2)}) copy-start(bf16[8,33280]{1,0:T(8,128)(2,1)} %param.4) | copy-start | bytes 1597444
  1.4 0.7 %copy-start.1 = (s32[8]{0:T(128)S(1)}, s32[8]{0:T(128)}, u32[]{:S(2)}) copy-start(s32[8]{0:T(128)} %chan_hbm.1) | copy-start | bytes 100
